TPU v7x, 128 devices: a whole 4x4x4 slice. The times are simulated.
128 devices in a mesh: pts: 4 (over x_lo, core), comp: 32 (over x_hi, y, z).
Axes of the slice: x: 4 (x_hi: 2, x_lo: 2; x = x_hi * 2 + x_lo), y: 4, z: 4, core: 2. Of those that a mesh axis runs over, the one named last changes fastest.
Arguments:
- points: bfloat16 [1536, 512], P(('pts', 'comp')), may hold values from -28 to 28
- centres: bfloat16 [2048, 512], P('comp'), may hold values from -5 to 5
- whitening: bfloat16 [2048, 512, 512], P('comp', 'pts'), as said below
- log_prior: float32 [2048], P('comp'), may hold values from -4 to 4
Outputs:
- counts: float32 [2048], P('comp')
- first_moments: float32 [2048, 512], P('comp')
- second_moments: float32 [2048, 512, 512], P('comp', 'pts')
Inputs may be any that keep to these rules, and one draw needn't show every extreme that they name: Each whitening[k] is lower triangular with diagonal entries between 0.69 and 2.82.
All inputs are finite; a program needn't handle non-finite values.
Results may differ from a plain program's by a relative error of at most 0.0029.
Values may be sent and summed in bfloat16 or wider, within the bound.
No kernel may reach another device: no remote copies, remote signals or barrier semaphores. Data moves between devices by JAX's collectives and lax.ppermute only.
A program may use at most 128 MiB of HBM per device.

v0:
```python
import jax
import jax.numpy as jnp
from jax import lax
from jax.sharding import PartitionSpec as P

D = 512


anneal_beta = 1.25


def normalise(partial_total, prior_col):
    logits = anneal_beta * (prior_col - partial_total / D)
    row_peak = lax.pmax(jnp.max(logits, axis=0), "comp")
    expo_vals = jnp.exp(logits - row_peak[None, :])
    row_total = lax.psum(jnp.sum(expo_vals, axis=0), "comp")
    return (expo_vals / row_total[None, :]).astype(jnp.bfloat16)


def body(points, centres, whitening, log_prior):
    gathered = lax.all_gather(points, ("pts", "comp"), axis=0, tiled=True)
    comp_here = whitening.shape[0]
    band_rows = whitening.shape[1]
    total_points = gathered.shape[0]
    band_start = lax.axis_index("pts") * band_rows
    block_count = comp_here // 8
    factor_blocks = whitening.reshape(block_count, 8, band_rows, D)
    centre_blocks = centres.reshape(block_count, 8, D)

    def block_term(pair):
        factor, centre = pair
        offset = jnp.einsum("kqd,kd->kq", factor, centre, preferred_element_type=jnp.float32)
        whitened = (
            jnp.einsum("kqd,nd->kqn", factor, gathered, preferred_element_type=jnp.float32)
            - offset[:, :, None]
        )
        square_cols = lax.dynamic_slice_in_dim(factor, band_start, band_rows, 2)
        diag_vals = jnp.diagonal(square_cols, axis1=1, axis2=2).astype(jnp.float32)
        return (
            0.5 * jnp.sum(whitened * whitened, axis=1)
            - jnp.sum(jnp.log(diag_vals), axis=1)[:, None]
        )

    partial_term = lax.map(block_term, (factor_blocks, centre_blocks)).reshape(
        comp_here, total_points
    )
    prior_col = log_prior[:, None]
    summed = lax.psum(partial_term, "pts")
    responsibility = normalise(summed, prior_col)
    counts = jnp.sum(responsibility.astype(jnp.float32), axis=1)
    first_moments = jnp.dot(responsibility, gathered, preferred_element_type=jnp.float32)
    band_points = lax.dynamic_slice_in_dim(gathered, band_start, band_rows, 1).T.astype(jnp.float32)

    def block_second(resp_block):
        weighted = (resp_block.astype(jnp.float32)[:, None, :] * band_points[None, :, :]).astype(
            jnp.bfloat16
        )
        return jnp.einsum("kqn,nd->kqd", weighted, gathered, preferred_element_type=jnp.float32)

    second_moments = lax.map(block_second, responsibility.reshape(block_count, 8, total_points))
    return (counts, first_moments, second_moments.reshape(comp_here, band_rows, D))


def solution(mesh):
    in_specs = (P(("pts", "comp"), None), P("comp", None), P("comp", "pts", None), P("comp"))
    out_specs = (P("comp"), P("comp", None), P("comp", "pts", None))
    return jax.shard_map(body, mesh=mesh, in_specs=in_specs, out_specs=out_specs, check_vma=False)
```

profile of v0, /device:TPU:0, one launch (start us, length us, event | category | flops | bytes accessed | tf_op | source)
XLA Modules:
  0.0 677.8 jit_solution(2913701126033206041)
XLA Ops:
  8.0 305.8 %all-gather.3.cloned.1.call-done = bf16[128,12,512]{2,1,0:T(8,128)(2,1)} async-done(((bf16[1,12,512]{2,1,0:T(8,128)(2,1)}), bf16[128,12,512]{2,1,0:T(8,128)(2,1)}) %all-gather.3.cloned.1.call-update) | async-done | bytes 1572880 | tf_op jit(solution)/shard_map/all_gather | solution.py:21
  313.8 2.5 reshape.85
  316.3 99.1 %while.23 = (s32[]{:T(128)}, f32[8,8,1536]{2,1,0:T(8,128)}, bf16[8,8,128,512]{3,2,1,0:T(8,128)(2,1)}, bf16[1536,512]{1,0:T(8,128)(2,1)S(1)}, bf16[8,8,512]{2,1,0...) while((s32[]{:T(128)}, f32[8,8,1536]{2,1,0:T(8,128)}, bf16[8,8,128,512]{3,2,1,0:T(8,128)(2,1)}, ...), condition=%wide.region_3.4_spmd, body=%wide.region_0.3_spmd.sunk | while | flops 1616394752 | bytes 4908217 | solution.py:44
  318.6 3.1 multiply_reduce_fusion.2
  322.9 3.1 copy.20
  331.0 3.1 multiply_reduce_fusion.2
  335.3 3.1 copy.20
  343.3 3.1 multiply_reduce_fusion.2
  347.6 3.1 copy.20
  355.7 3.1 multiply_reduce_fusion.2
  360.0 3.1 copy.20
  363.1 2.0 gather_fusion
  368.1 3.1 multiply_reduce_fusion.2
  372.4 3.1 copy.20
  380.5 3.1 multiply_reduce_fusion.2
  384.8 3.1 copy.20
  392.9 3.1 multiply_reduce_fusion.2
  397.2 3.1 copy.20
  405.3 3.1 multiply_reduce_fusion.2
  409.5 3.1 copy.20
  415.7 38.1 %all-reduce.2.cloned.1.call-done = f32[64,1536]{1,0:T(8,128)} async-done(((f32[64,1536]{1,0:T(8,128)}), f32[64,1536]{1,0:T(8,128)}) %all-reduce.2.cloned.1.call-update) | async-done | bytes 393232 | tf_op jit(solution)/shard_map/psum | solution.py:48
  455.0 97.2 %pmax.7 = f32[1536]{0:T(1024)S(1)} all-reduce(f32[1536]{0:T(1024)S(1)} %fusion.15), channel_id=1, replica_groups=mesh['pts'=4,'comp'=32] {'comp'}, use_global_device_ids=true, to_apply=%region_6.7 | all-reduce | flops 1536 | bytes 12288 | tf_op jit(solution)/shard_map/pmax | solution.py:14
  553.3 90.0 %psum.15 = f32[1536]{0:T(1024)S(1)} all-reduce(f32[1536]{0:T(1024)S(1)} %fusion.14), channel_id=1, replica_groups=mesh['pts'=4,'comp'=32] {'comp'}, use_global_device_ids=true, to_apply=%region_8.9 | all-reduce | flops 1536 | bytes 12288 | tf_op jit(solution)/shard_map/psum | solution.py:16
  646.1 24.9 %while.24 = (s32[]{:T(128)}, f32[8,8,128,512]{3,2,1,0:T(8,128)}, bf16[8,8,1536]{2,1,0:T(8,128)(2,1)S(1)}, f32[128,1536]{1,0:T(8,128)S(1)}, bf16[1536,512]{1,0:T(8,128)(2,1)S(1)}, /*index=5*/s32[]{:T(128)}) while((s32[]{:T(128)}, f32[8,8,128,512]{3,2,1,0:T(8,128)}, bf16[8,8,1536]{2,1,0:T(8,128)(2,1)S(1)}, f32[128,1536]{1,0:T(8,128)S(1)}, ...), condition=%wide.region_11.12_spmd, body=%wide.region_10.11_spmd.sunk | while | flops 1613770752 | bytes 4579913 | solution.py:60
  646.1 3.1 bitcast_dynamic-update-slice_fusion.2
  649.2 3.1 bitcast_dynamic-update-slice_fusion.2
  652.4 3.1 bitcast_dynamic-update-slice_fusion.2
  655.5 3.1 bitcast_dynamic-update-slice_fusion.2
  658.6 3.1 bitcast_dynamic-update-slice_fusion.2
  661.7 3.1 bitcast_dynamic-update-slice_fusion.2
  664.8 3.1 bitcast_dynamic-update-slice_fusion.2
  667.9 3.1 bitcast_dynamic-update-slice_fusion.2
  (77 shorter events, 53.9 us)
Async XLA Ops:
  7.2 306.6 %all-gather.3.cloned.1.call-start = ((), (), s32[]{:S(2)}) async-start(), calls=%async_computation.1 | async-start | bytes 2113536 | tf_op jit(solution)/shard_map/all_gather | solution.py:21
  7.9 446.0 %all-reduce.2.cloned.1.call-start = ((), (), s32[]{:S(2)}) async-start(), calls=%async_computation | async-start | bytes 786432 | tf_op jit(solution)/shard_map/psum | solution.py:48
  316.3 137.6 %copy-start = (f32[64]{0:T(128)S(1)}, f32[64]{0:T(128)}, u32[]{:S(2)}) copy-start(f32[64]{0:T(128)} %param.11) | copy-start | bytes 772
Sparse Core Ops, SparseCore 0:
  9.7 304.0 all-gather.2
  415.5 38.3 all-reduce.1
where the time goes:
time: 680 us; the launch traced here: 678 us
  waiting for transfers between devices  345 us (51%)
  blocking collectives  187 us (28%)
  matrix products  63.2 us (9%)
  local copies, waits for them, and re-layouts  58.3 us (9%)
  between operations  14.1 us (2%)
  other arithmetic  10.1 us (1%)
    all_gather x1, waiting for transfers between devices, body(): gathered = lax.all_gather(points, ('pts', 'comp'), axis=0, tiled=True)  306 us
    pmax x1, blocking collectives, normalise(): row_peak = lax.pmax(jnp.max(logits, axis=0), 'comp')  97.2 us
    psum x1, blocking collectives, normalise(): row_total = lax.psum(jnp.sum(expo_vals, axis=0), 'comp')  90 us
    psum x1, waiting for transfers between devices, body(): summed = lax.psum(partial_term, 'pts')  38.1 us
    dynamic_slice x16, local copies, waits for them, and re-layouts, block_term(): square_cols = lax.dynamic_slice_in_dim(factor, band_start, band_rows, 2)  34.1 us
    dot_general x8, matrix products, block_second(): jnp.einsum('kqn,nd->kqd', weighted, gathered, preferred_element_type=jnp....  24.8 us
    dot_general x8, matrix products, block_term(): jnp.einsum('kqd,nd->kqn', factor, gathered, preferred_element_type=jnp.fl...  24.7 us
    gather x8, local copies, waits for them, and re-layouts, block_term(): diag_vals = jnp.diagonal(square_cols, axis1=1, axis2=2).astype(jnp.float32)  15.9 us
  transfers between devices with their start and end apart: 2, of which 2 were waited for; matrix products, arithmetic and copies ran while one was open for 0% of the time, Pallas kernels for 0%

commit v1 on v0

v1 whole, which is shorter than its diff:
```python
import functools

import jax
import jax.numpy as jnp
from jax import lax
from jax.experimental import pallas as pl
from jax.experimental.pallas import tpu as pltpu
from jax.sharding import Mesh, PartitionSpec as P

D = 512
HALF = D // 2
BETA = 1.25
NT = (((1,), (1,)), ((), ()))
VMEM = 60 << 20
f32 = jnp.float32
bf16 = jnp.bfloat16
ALL = ("xl", "c", "xh", "y", "z")
CHIPS = ("xl", "xh", "y", "z")
COMP = ("xh", "y", "z")


def prep_kernel(pos, w_ref, wd_ref, c_ref, off_ref, ld_ref, *, kb):
    q = w_ref.shape[1]
    row = lax.broadcasted_iota(jnp.int32, (q, q), 0)
    eye = row == lax.broadcasted_iota(jnp.int32, (q, q), 1)
    for k in range(kb):
        prod = w_ref[k].astype(f32) * c_ref[k : k + 1, :].astype(f32)
        off_ref[0, :, k : k + 1] = jnp.sum(prod, axis=1, keepdims=True)
        diag = jnp.sum(jnp.where(eye, wd_ref[k].astype(f32), 0.0), axis=0, keepdims=True)
        total = jnp.sum(jnp.log(diag), axis=1, keepdims=True)
        ld_ref[k : k + 1, :] = jnp.broadcast_to(total, (1, 128))


def prep(pos, w, cen, kb=8):
    k, q, _ = w.shape
    spec = pltpu.PrefetchScalarGridSpec(
        num_scalar_prefetch=1,
        grid=(k // kb,),
        in_specs=[
            pl.BlockSpec((kb, q, D), lambda i, p: (i, 0, 0)),
            pl.BlockSpec((kb, q, q), lambda i, p: (i, 0, p[2])),
            pl.BlockSpec((kb, D), lambda i, p: (i, 0)),
        ],
        out_specs=[
            pl.BlockSpec((1, q, kb), lambda i, p: (i, 0, 0)),
            pl.BlockSpec((kb, 128), lambda i, p: (i, 0)),
        ],
    )
    return pl.pallas_call(
        functools.partial(prep_kernel, kb=kb),
        grid_spec=spec,
        out_shape=[
            jax.ShapeDtypeStruct((k // kb, q, kb), f32),
            jax.ShapeDtypeStruct((k, 128), f32),
        ],
        cost_estimate=pl.CostEstimate(flops=8_000_000, bytes_accessed=10_500_000, transcendentals=8192),
        name="prep",
    )(pos, w, w, cen)


def dist_kernel(pos, w_ref, off_ref, ld_ref, xa_ref, xb_ref, o_ref, *, kb, nt, mine):
    q = w_ref.shape[1]
    n = o_ref.shape[1]
    c = pos[0]
    side = c if mine else 1 - c
    ca = pl.multiple_of(c * HALF, HALF)
    cb = pl.multiple_of((1 - c) * HALF, HALF)
    wa = w_ref[:, :, pl.ds(ca, HALF)].reshape(kb * q, HALF)
    wb = w_ref[:, :, pl.ds(cb, HALF)].reshape(kb * q, HALF)
    for t in range(n // nt):
        rows = pl.ds(pl.multiple_of(side * n + t * nt, nt), nt)
        y = lax.dot_general(wa, xa_ref[rows, :], NT, preferred_element_type=f32)
        y = y + lax.dot_general(wb, xb_ref[rows, :], NT, preferred_element_type=f32)
        for k in range(kb):
            u = y[k * q : (k + 1) * q] - off_ref[0, :, k : k + 1]
            part = 0.5 * jnp.sum(u * u, axis=0, keepdims=True) - ld_ref[k : k + 1, :1]
            o_ref[k : k + 1, t * nt : (t + 1) * nt] = part


def dist(pos, w, off, ld, xa, xb, mine, kb=8, nt=256):
    k, q, _ = w.shape
    n = xa.shape[0] // 2
    spec = pltpu.PrefetchScalarGridSpec(
        num_scalar_prefetch=1,
        grid=(k // kb,),
        in_specs=[
            pl.BlockSpec((kb, q, D), lambda i, p: (i, 0, 0)),
            pl.BlockSpec((1, q, kb), lambda i, p: (i, 0, 0)),
            pl.BlockSpec((kb, 128), lambda i, p: (i, 0)),
            pl.BlockSpec((2 * n, HALF), lambda i, p: (0, 0)),
            pl.BlockSpec((2 * n, HALF), lambda i, p: (0, 0)),
        ],
        out_specs=pl.BlockSpec((kb, n), lambda i, p: (i, 0)),
    )
    return pl.pallas_call(
        functools.partial(dist_kernel, kb=kb, nt=nt, mine=mine),
        grid_spec=spec,
        out_shape=jax.ShapeDtypeStruct((k, n), f32),
        compiler_params=pltpu.CompilerParams(vmem_limit_bytes=VMEM),
        cost_estimate=pl.CostEstimate(
            flops=2 * k * q * D * n, bytes_accessed=2 * k * q * D + 4 * n * D + 4 * k * n, transcendentals=0
        ),
        name="dist_keep" if mine else "dist_send",
    )(pos, w, off, ld, xa, xb)


def band_kernel(pos, xa_ref, xb_ref, o_ref):
    c, xl = pos[0], pos[1]
    cols = pl.ds(pl.multiple_of(c * 128, 128), 128)

    @pl.when(c == xl)
    def _():
        o_ref[...] = xa_ref[:, cols].astype(f32).T.astype(bf16)

    @pl.when(c != xl)
    def _():
        o_ref[...] = xb_ref[:, cols].astype(f32).T.astype(bf16)


def band(pos, xa, xb):
    n = xa.shape[0]
    spec = pltpu.PrefetchScalarGridSpec(
        num_scalar_prefetch=1,
        grid=(1,),
        in_specs=[pl.BlockSpec((n, HALF), lambda i, p: (0, 0))] * 2,
        out_specs=pl.BlockSpec((128, n), lambda i, p: (0, 0)),
    )
    return pl.pallas_call(
        band_kernel,
        grid_spec=spec,
        out_shape=jax.ShapeDtypeStruct((128, n), bf16),
        cost_estimate=pl.CostEstimate(flops=0, bytes_accessed=2_000_000, transcendentals=0),
        name="band",
    )(pos, xa, xb)


def sec_kernel(pos, ra_ref, rb_ref, xt_ref, xa_ref, xb_ref, o_ref, fm_ref, ct_ref, wt_ref, *, kb):
    q = xt_ref.shape[0]
    h = ra_ref.shape[1]
    c = pos[0]
    for r_ref, side in ((ra_ref, c), (rb_ref, 1 - c)):
        cols = pl.ds(pl.multiple_of(side * h, 128), h)
        xv = xt_ref[:, cols]
        for k in range(kb):
            wt_ref[k * q : (k + 1) * q, cols] = xv * r_ref[k : k + 1, :]
        wt_ref[kb * q : kb * q + kb, cols] = r_ref[...]
    ra_sum = jnp.sum(ra_ref[...].astype(f32), axis=1, keepdims=True)
    ct_ref[...] = ra_sum + jnp.sum(rb_ref[...].astype(f32), axis=1, keepdims=True)
    wt = wt_ref[...]
    for x_ref, side in ((xa_ref, c), (xb_ref, 1 - c)):
        cols = pl.ds(pl.multiple_of(side * HALF, HALF), HALF)
        y = jnp.dot(wt, x_ref[...], preferred_element_type=f32)
        o_ref[:, :, cols] = y[: kb * q].reshape(kb, q, HALF)
        fm_ref[:, cols] = y[kb * q : kb * q + kb]


def sec(pos, ra, rb, xt, xa, xb, kb=16):
    k, h = ra.shape
    n = xa.shape[0]
    q = xt.shape[0]
    spec = pltpu.PrefetchScalarGridSpec(
        num_scalar_prefetch=1,
        grid=(k // kb,),
        in_specs=[
            pl.BlockSpec((kb, h), lambda i, p: (i, 0)),
            pl.BlockSpec((kb, h), lambda i, p: (i, 0)),
            pl.BlockSpec((q, n), lambda i, p: (0, 0)),
            pl.BlockSpec((n, HALF), lambda i, p: (0, 0)),
            pl.BlockSpec((n, HALF), lambda i, p: (0, 0)),
        ],
        out_specs=[
            pl.BlockSpec((kb, q, D), lambda i, p: (i, 0, 0)),
            pl.BlockSpec((kb, D), lambda i, p: (i, 0)),
            pl.BlockSpec((kb, 1), lambda i, p: (i, 0)),
        ],
        scratch_shapes=[pltpu.VMEM((kb * q + kb, n), bf16)],
    )
    return pl.pallas_call(
        functools.partial(sec_kernel, kb=kb),
        grid_spec=spec,
        out_shape=[
            jax.ShapeDtypeStruct((k, q, D), f32),
            jax.ShapeDtypeStruct((k, D), f32),
            jax.ShapeDtypeStruct((k, 1), f32),
        ],
        compiler_params=pltpu.CompilerParams(vmem_limit_bytes=VMEM),
        cost_estimate=pl.CostEstimate(
            flops=2 * k * q * D * n, bytes_accessed=4 * k * q * D + 4 * n * D, transcendentals=0
        ),
        name="sec",
    )(pos, ra, rb, xt, xa, xb)


def swap(x, axis):
    return lax.ppermute(x, axis, [(0, 1), (1, 0)])


def body(points, centres, whitening, log_prior):
    c, xl = lax.axis_index("c"), lax.axis_index("xl")
    pos = jnp.stack([c, xl, xl * 2 + c]).astype(jnp.int32)
    chips = lax.psum(1, CHIPS)
    groups = lax.psum(1, COMP)

    cols = lax.all_to_all(points, "c", 1, 0, tiled=True)
    m = cols.shape[0]
    xa = lax.all_to_all(jnp.broadcast_to(cols[None], (chips, m, HALF)), CHIPS, 0, 0, tiled=True)
    xa = xa.reshape(chips * m, HALF)
    xb = swap(xa, "c")

    off, ld = prep(pos, whitening, centres)
    send = dist(pos, whitening, off, ld, xa, xb, mine=False)
    got = swap(send, "c")
    keep = dist(pos, whitening, off, ld, xa, xb, mine=True)
    chip_part = keep + got
    total = chip_part + swap(chip_part, "xl")
    xt = band(pos, xa, xb)

    logits = BETA * (log_prior[:, None] - total / D)
    peak = jnp.max(logits, axis=0)
    lse = peak + jnp.log(jnp.sum(jnp.exp(logits - peak[None, :]), axis=0))
    h = lse.shape[0]
    lanes = lse.reshape(1, h // 128, 128)
    others = lax.all_to_all(jnp.broadcast_to(lanes, (groups, h // 128, 128)), COMP, 0, 0, tiled=True)
    top = jnp.max(others, axis=0)
    norm = (top + jnp.log(jnp.sum(jnp.exp(others - top[None]), axis=0))).reshape(h)
    ra = jnp.exp(logits - norm[None, :]).astype(bf16)
    rb = swap(ra, "c")
    second, first, counts = sec(pos, ra, rb, xt, xa, xb)
    return counts[:, 0], first, second


def solution(mesh):
    sizes = (2, 2, 2, 4, 4)
    fine = Mesh(mesh.devices.reshape(sizes), ALL)
    band_axes = ("xl", "c")
    in_specs = (P(ALL, None), P(COMP, None), P(COMP, band_axes, None), P(COMP))
    out_specs = (P(COMP), P(COMP, None), P(COMP, band_axes, None))
    return jax.shard_map(body, mesh=fine, in_specs=in_specs, out_specs=out_specs, check_vma=False)
```

time: 680 us -> 119 us (0.17)
  the two profiles are of different devices: /device:TPU:0 before, /device:TPU:1 now
where the time goes in v1:
time: 119 us; the launch traced here: 117 us
  Pallas kernels  57 us (48%)
  blocking collectives  43.1 us (36%)
  waiting for transfers between devices  6.03 us (5%)
  starting transfers between devices  5.07 us (4%)
  other arithmetic  3.22 us (3%)
  local copies, waits for them, and re-layouts  2.35 us (2%)
    all_to_all x1, blocking collectives, body(): lax.all_to_all(jnp.broadcast_to(cols[None], (chips, m, HALF)), CHIPS, 0,...  25.8 us
    pallas_call x2, Pallas kernels, dist(): pl.pallas_call(functools.partial(dist_kernel, kb=kb, nt=nt, mine=mine), g...  24.5 us
    pallas_call x1, Pallas kernels, sec(): pl.pallas_call(functools.partial(sec_kernel, kb=kb), grid_spec=spec, out_...  20.6 us
    all_to_all x1, blocking collectives, body(): lax.all_to_all(jnp.broadcast_to(lanes, (groups, h // 128, 128)), COMP, 0,...  12.5 us
    pallas_call x1, Pallas kernels, prep(): pl.pallas_call(functools.partial(prep_kernel, kb=kb), grid_spec=spec, out...  8.97 us
    ppermute x4, waiting for transfers between devices, swap(): return lax.ppermute(x, axis, [(0, 1), (1, 0)])  6.03 us
    ppermute x4, starting transfers between devices, swap(): return lax.ppermute(x, axis, [(0, 1), (1, 0)])  5.07 us
    all_to_all x1, blocking collectives, body(): cols = lax.all_to_all(points, 'c', 1, 0, tiled=True)  4.76 us
  transfers between devices with their start and end apart: 4, of which 1 were waited for; matrix products, arithmetic and copies ran while one was open for 0% of the time, Pallas kernels for 21%

profile of v1, /device:TPU:1, one launch (start us, length us, event | category | flops | bytes accessed | tf_op | source)
XLA Modules:
  0.0 117.5 jit_solution(6319832074572882878)
XLA Ops:
  0.6 0.7 all_to_all.18
  1.4 4.8 %all_to_all.26 = bf16[12,2,256]{2,0,1:T(8,128)(2,1)S(1)} all-to-all(bf16[12,2,256]{2,0,1:T(8,128)(2,1)S(1)} %copy.9), channel_id=1, replica_groups=mesh['xl'=2,'c'=2,'xh'=2,'y'=4,'z'=4] {'c'}, dimensions={1} | all-to-all | bytes 24576 | tf_op jit(solution)/shard_map/all_to_all | solution.py:204
  6.1 0.1 broadcast_in_dim.7
  6.2 25.8 %all_to_all.27 = bf16[64,24,256]{2,1,0:T(8,128)(2,1)S(1)} all-to-all(bf16[64,24,256]{2,1,0:T(8,128)(2,1)S(1)} %broadcast_in_dim.7), channel_id=1, replica_groups=mesh['xl'=2,'c'=2,'xh'=2,'y'=4,'z'=4] {'xl','xh','y','z'}, dimensions={0} | all-to-all | bytes 1572864 | tf_op jit(solution)/shard_map/all_to_all | solution.py:206
  32.0 0.0 copy-start
  32.0 2.2 %collective-permute-start = (bf16[1536,256]{1,0:T(8,128)(2,1)S(1)}, bf16[1536,256]{1,0:T(8,128)(2,1)S(1)}, u32[]{:S(2)}, u32[]{:S(2)}) collective-permute-start(bf16[1536,256]{1,0:T(8,128)(2,1)S(1)} %bitcast.9), channel_id=1, source_target_pairs={{0,32},{32,0},{1,33},{33,1},{2,34},{34,2},{3,35},{35,3},{4,36},{36... | collective-permute-start | bytes 2359304 | tf_op jit(solution)/shard_map/ppermute | solution.py:195
  34.2 0.6 pad_add_fusion.pos
  34.8 9.0 %prep.1 = (f32[8,128,8]{2,1,0:T(8,128)}, f32[64,128]{1,0:T(8,128)}) custom-call(s32[3]{0:T(128)} %pad_add_fusion.pos, bf16[64,128,512]{2,1,0:T(8,128)(2,1)} %w_ref.5, bf16[64,128,512]{2,1,0:T(8,128)(2,1)} %w_ref.5, bf16[64,512]{1,0:T(8,128)(2,1)} %c_ref.1), custom_call_target="tpu_custom_call" | custom-call | flops 8000000 | bytes 10500000 | tf_op jit(solution)/shard_map/prep/pallas_call | solution.py:49
  43.8 0.0 collective-permute-done.xb_ref
  43.8 0.0 copy-start.1
  43.8 0.0 copy-done
  43.8 0.9 copy-done.1
  44.7 12.3 %dist_send.1 = f32[64,768]{1,0:T(8,128)} custom-call(s32[3]{0:T(128)} %pad_add_fusion.pos, bf16[64,128,512]{2,1,0:T(8,128)(2,1)} %w_ref.5, f32[8,128,8]{2,1,0:T(8,128)} %get-tuple-element.8.off_ref, f32[64,128]{1,0:T(8,128)} %get-tuple-element.9.ld_ref, bf16[1536,256]{1,0:T(8,128)(2,1)} %bitcast.10, bf16[1536,256]{1,0:T(8,128)(2,1)} %copy-done.1), custom_call_target="tpu_custom_call" | custom-call | flops 6442450944 | bytes 10158080 | tf_op jit(solution)/shard_map/dist_send/pallas_call | solution.py:95
  56.9 0.0 collective-permute-start.1
  57.0 12.2 %dist_keep.1 = f32[64,768]{1,0:T(8,128)} custom-call(s32[3]{0:T(128)} %pad_add_fusion.pos, bf16[64,128,512]{2,1,0:T(8,128)(2,1)} %w_ref.5, f32[8,128,8]{2,1,0:T(8,128)} %get-tuple-element.8.off_ref, f32[64,128]{1,0:T(8,128)} %get-tuple-element.9.ld_ref, bf16[1536,256]{1,0:T(8,128)(2,1)} %bitcast.11, bf16[1536,256]{1,0:T(8,128)(2,1)} %copy-done.1), custom_call_target="tpu_custom_call" | custom-call | flops 6442450944 | bytes 10158080 | tf_op jit(solution)/shard_map/dist_keep/pallas_call | solution.py:95
  69.2 0.0 collective-permute-done.1
  69.2 1.0 add.30
  70.2 0.1 collective-permute-start.2
  70.3 6.0 %collective-permute-done.2 = f32[64,768]{1,0:T(8,128)S(1)} collective-permute-done((f32[64,768]{1,0:T(8,128)S(1)}, f32[64,768]{1,0:T(8,128)S(1)}, u32[]{:S(2)}, u32[]{:S(2)}) %collective-permute-start.2) | collective-permute-done | bytes 196640 | tf_op jit(solution)/shard_map/ppermute | solution.py:195
  76.3 0.0 copy-done.3
  76.3 0.1 fusion
  76.4 0.1 exponential_reduce_fusion
  76.5 12.5 %all_to_all.28 = f32[32,6,128]{2,1,0:T(8,128)S(1)} all-to-all(f32[32,6,128]{2,1,0:T(8,128)S(1)} %broadcast_in_dim.8), channel_id=1, replica_groups=mesh['xl'=2,'c'=2,'xh'=2,'y'=4,'z'=4] {'xh','y','z'}, dimensions={0} | all-to-all | bytes 196608 | tf_op jit(solution)/shard_map/all_to_all | solution.py:223
  89.1 0.0 copy-start.2
  89.1 2.8 %collective-permute-start.3 = (bf16[64,768]{1,0:T(8,128)(2,1)S(1)}, bf16[64,768]{1,0:T(8,128)(2,1)S(1)}, u32[]{:S(2)}, u32[]{:S(2)}) collective-permute-start(bf16[64,768]{1,0:T(8,128)(2,1)S(1)} %exponential_convert_fusion.ra_ref), channel_id=1, source_target_pairs={{0,32},{32,0},{1,33},{33,1},{2,34},{34,2},{3,35},{35,3},{4,36},{36... | collective-permute-start | bytes 294920 | tf_op jit(solution)/shard_map/ppermute | solution.py:195
  91.8 2.9 %band.1.xt_ref = bf16[128,1536]{1,0:T(8,128)(2,1)} custom-call(s32[3]{0:T(128)} %pad_add_fusion.pos, bf16[1536,256]{1,0:T(8,128)(2,1)} %bitcast.12, bf16[1536,256]{1,0:T(8,128)(2,1)} %copy-done.1), custom_call_target="tpu_custom_call" | custom-call | bytes 2000000 | tf_op jit(solution)/shard_map/band/pallas_call | solution.py:128
  94.8 0.0 collective-permute-done.3.rb_ref
  94.8 0.0 copy-done.2
  94.8 0.0 copy-start.4
  94.8 0.6 copy-done.4
  95.4 20.6 %sec.1 = (f32[64,128,512]{2,1,0:T(8,128)}, f32[64,512]{1,0:T(8,128)}, f32[64,1]{1,0:T(8,128)}) custom-call(s32[3]{0:T(128)} %pad_add_fusion.pos, bf16[64,768]{1,0:T(8,128)(2,1)} %copy-done.2, bf16[64,768]{1,0:T(8,128)(2,1)} %copy-done.4, bf16[128,1536]{1,0:T(8,128)(2,1)} %band.1.xt_ref, bf16[1536,256]{1,0:T(8,128)(2,1)} %bitcast.13, bf16[1536,256]{1,0:T(8,128)(2,1)} %copy-done.1), custom_call_target="tpu_custom_call" | custom-call | flops 12884901888 | bytes 19922944 | tf_op jit(solution)/shard_map/sec/pallas_call | solution.py:178
  116.1 1.4 %reduce = f32[64]{0:T(128)} reduce(f32[64,1]{1,0:T(8,128)} %get-tuple-element.10, f32[]{:T(128)} %constant.22), dimensions={1}, to_apply=%get-tuple-element.10.reduce_sub_computation | reduce | bytes 516 | tf_op jit(solution)/shard_map/sec/pallas_call | solution.py:178
  (9 shorter events, 0.2 us)
Async XLA Ops:
  32.0 11.7 %copy-start = (bf16[64,24,256]{2,1,0:T(8,128)(2,1)}, bf16[64,24,256]{2,1,0:T(8,128)(2,1)S(1)}, u32[]{:S(2)}) copy-start(bf16[64,24,256]{2,1,0:T(8,128)(2,1)S(1)} %all_to_all.27) | copy-start | bytes 2359300
  32.0 11.7 %collective-permute-start = (bf16[1536,256]{1,0:T(8,128)(2,1)S(1)}, bf16[1536,256]{1,0:T(8,128)(2,1)S(1)}, u32[]{:S(2)}, u32[]{:S(2)}) collective-permute-start(bf16[1536,256]{1,0:T(8,128)(2,1)S(1)} %bitcast.9), channel_id=1, source_target_pairs={{0,32},{32,0},{1,33},{33,1},{2,34},{34,2},{3,35},{35,3},{4,36},{36... | collective-permute-start | bytes 2359304 | tf_op jit(solution)/shard_map/ppermute | solution.py:195
  43.8 0.9 copy-start.1
  56.9 19.4 %copy-start.3 = (f32[64]{0:T(128)S(1)}, f32[64]{0:T(128)}, u32[]{:S(2)}) copy-start(f32[64]{0:T(128)} %param.7) | copy-start | bytes 772
  56.9 12.3 %collective-permute-start.1 = (f32[64,768]{1,0:T(8,128)}, f32[64,768]{1,0:T(8,128)S(1)}, u32[]{:S(2)}, u32[]{:S(2)}) collective-permute-start(f32[64,768]{1,0:T(8,128)} %dist_send.1), channel_id=1, source_target_pairs={{0,32},{32,0},{1,33},{33,1},{2,34},{34,2},{3,35},{35,3},{4,36},{36... | collective-permute-start | bytes 589832 | tf_op jit(solution)/shard_map/ppermute | solution.py:195
  70.2 6.1 %collective-permute-start.2 = (f32[64,768]{1,0:T(8,128)S(1)}, f32[64,768]{1,0:T(8,128)S(1)}, u32[]{:S(2)}, u32[]{:S(2)}) collective-permute-start(f32[64,768]{1,0:T(8,128)S(1)} %add.30), channel_id=1, source_target_pairs={{0,64},{64,0},{1,65},{65,1},{2,66},{66,2},{3,67},{67,3},{4,68},{68... | collective-permute-start | bytes 589832 | tf_op jit(solution)/shard_map/ppermute | solution.py:195
  89.1 5.7 %copy-start.2 = (bf16[64,768]{1,0:T(8,128)(2,1)}, bf16[64,768]{1,0:T(8,128)(2,1)S(1)}, u32[]{:S(2)}) copy-start(bf16[64,768]{1,0:T(8,128)(2,1)S(1)} %exponential_convert_fusion.ra_ref) | copy-start | bytes 294916
  89.1 5.7 %collective-permute-start.3 = (bf16[64,768]{1,0:T(8,128)(2,1)S(1)}, bf16[64,768]{1,0:T(8,128)(2,1)S(1)}, u32[]{:S(2)}, u32[]{:S(2)}) collective-permute-start(bf16[64,768]{1,0:T(8,128)(2,1)S(1)} %exponential_convert_fusion.ra_ref), channel_id=1, source_target_pairs={{0,32},{32,0},{1,33},{33,1},{2,34},{34,2},{3,35},{35,3},{4,36},{36... | collective-permute-start | bytes 294920 | tf_op jit(solution)/shard_map/ppermute | solution.py:195
  94.8 0.6 copy-start.4

commit v2 on v1

v2 whole, which is shorter than its diff:
```python
import functools

import jax
import jax.numpy as jnp
from jax import lax
from jax.experimental import pallas as pl
from jax.experimental.pallas import tpu as pltpu
from jax.sharding import Mesh, PartitionSpec as P

D = 512
HALF = D // 2
BETA = 1.25
NT = (((1,), (1,)), ((), ()))
VMEM = 24 << 20
STREAM = 24 << 20
KB_DIST = 16
f32 = jnp.float32
bf16 = jnp.bfloat16
ALL = ("xl", "c", "xh", "y", "z")
CHIPS = ("xl", "xh", "y", "z")
COMP = ("xh", "y", "z")


def prep_kernel(pos, w_ref, wd_ref, c_ref, off_ref, ld_ref, *, kb):
    q = w_ref.shape[1]
    row = lax.broadcasted_iota(jnp.int32, (q, q), 0)
    eye = row == lax.broadcasted_iota(jnp.int32, (q, q), 1)
    for k in range(kb):
        prod = w_ref[k].astype(f32) * c_ref[k : k + 1, :].astype(f32)
        off_ref[0, :, k : k + 1] = jnp.sum(prod, axis=1, keepdims=True)
        diag = jnp.sum(jnp.where(eye, wd_ref[k].astype(f32), 0.0), axis=0, keepdims=True)
        total = jnp.sum(jnp.log(diag), axis=1, keepdims=True)
        ld_ref[k : k + 1, :] = jnp.broadcast_to(total, (1, 128))


def prep(pos, w, cen, kb=8):
    k, q, _ = w.shape
    spec = pltpu.PrefetchScalarGridSpec(
        num_scalar_prefetch=1,
        grid=(k // kb,),
        in_specs=[
            pl.BlockSpec((kb, q, D), lambda i, p: (i, 0, 0)),
            pl.BlockSpec((kb, q, q), lambda i, p: (i, 0, p[2])),
            pl.BlockSpec((kb, D), lambda i, p: (i, 0)),
        ],
        out_specs=[
            pl.BlockSpec((1, q, kb), lambda i, p: (i, 0, 0)),
            pl.BlockSpec((kb, 128), lambda i, p: (i, 0)),
        ],
    )
    return pl.pallas_call(
        functools.partial(prep_kernel, kb=kb),
        grid_spec=spec,
        out_shape=[
            jax.ShapeDtypeStruct((k // kb, q, kb), f32),
            jax.ShapeDtypeStruct((k, 128), f32),
        ],
        compiler_params=pltpu.CompilerParams(vmem_limit_bytes=STREAM),
        cost_estimate=pl.CostEstimate(flops=8_000_000, bytes_accessed=10_500_000, transcendentals=8192),
        name="prep",
    )(pos, w, w, cen)


def dist_kernel(pos, wa_ref, wb_ref, off_ref, ld_ref, xa_ref, xb_ref, send_ref, keep_ref, *, kb, nt):
    q = wa_ref.shape[1]
    n = keep_ref.shape[1]
    c = pos[0]
    wa = wa_ref[...].reshape(kb * q, HALF)
    wb = wb_ref[...].reshape(kb * q, HALF)
    for o_ref, side in ((send_ref, 1 - c), (keep_ref, c)):
        for t in range(n // nt):
            rows = pl.ds(pl.multiple_of(side * n + t * nt, nt), nt)
            y = lax.dot_general(wa, xa_ref[rows, :], NT, preferred_element_type=f32)
            y = y + lax.dot_general(wb, xb_ref[rows, :], NT, preferred_element_type=f32)
            for k in range(kb):
                u = y[k * q : (k + 1) * q] - off_ref[k // 8, :, k % 8 : k % 8 + 1]
                part = 0.5 * jnp.sum(u * u, axis=0, keepdims=True) - ld_ref[k : k + 1, :1]
                o_ref[k : k + 1, t * nt : (t + 1) * nt] = part


def dist(pos, w, off, ld, xa, xb, kb=KB_DIST, nt=256):
    k, q, _ = w.shape
    n = xa.shape[0] // 2
    whole = pl.BlockSpec(memory_space=pltpu.VMEM)
    spec = pltpu.PrefetchScalarGridSpec(
        num_scalar_prefetch=1,
        grid=(k // kb,),
        in_specs=[
            pl.BlockSpec((kb, q, HALF), lambda i, p: (i, 0, p[0])),
            pl.BlockSpec((kb, q, HALF), lambda i, p: (i, 0, 1 - p[0])),
            pl.BlockSpec((kb // 8, q, 8), lambda i, p: (i, 0, 0)),
            pl.BlockSpec((kb, 128), lambda i, p: (i, 0)),
            whole,
            whole,
        ],
        out_specs=[pl.BlockSpec((kb, n), lambda i, p: (i, 0))] * 2,
    )
    return pl.pallas_call(
        functools.partial(dist_kernel, kb=kb, nt=nt),
        grid_spec=spec,
        out_shape=[jax.ShapeDtypeStruct((k, n), f32)] * 2,
        compiler_params=pltpu.CompilerParams(vmem_limit_bytes=STREAM),
        cost_estimate=pl.CostEstimate(
            flops=4 * k * q * D * n, bytes_accessed=2 * k * q * D + 4 * n * D + 8 * k * n, transcendentals=0
        ),
        name="dist",
    )(pos, w, w, off, ld, xa, xb)


def band_kernel(pos, xa_ref, xb_ref, o_ref):
    c, xl = pos[0], pos[1]
    h = o_ref.shape[1] // 2
    cols = pl.ds(pl.multiple_of(c * 128, 128), 128)
    for x_ref, here in ((xa_ref, c == xl), (xb_ref, c != xl)):

        @pl.when(here)
        def _():
            for t, side in enumerate((c, 1 - c)):
                rows = pl.ds(pl.multiple_of(side * h, h), h)
                o_ref[:, t * h : (t + 1) * h] = x_ref[rows, cols].astype(f32).T.astype(bf16)


def band(pos, xa, xb):
    n = xa.shape[0]
    whole = pl.BlockSpec(memory_space=pltpu.VMEM)
    spec = pltpu.PrefetchScalarGridSpec(num_scalar_prefetch=1, grid=(1,), in_specs=[whole] * 2, out_specs=whole)
    return pl.pallas_call(
        band_kernel,
        grid_spec=spec,
        out_shape=jax.ShapeDtypeStruct((128, n), bf16),
        compiler_params=pltpu.CompilerParams(vmem_limit_bytes=8 << 20),
        cost_estimate=pl.CostEstimate(flops=0, bytes_accessed=2_000_000, transcendentals=0),
        name="band",
    )(pos, xa, xb)


def sec_kernel(pos, ra_ref, rb_ref, xt_ref, xa_ref, xb_ref, o_ref, fm_ref, ct_ref, wt_ref, *, kb):
    q = xt_ref.shape[0]
    h = ra_ref.shape[1]
    c = pos[0]
    i, j = pl.program_id(0), pl.program_id(1)

    @pl.when((i == 0) & (j == 0))
    def _():
        ones = jnp.ones((8, h), bf16)
        total = lax.dot_general(ones, ra_ref[...], NT, preferred_element_type=f32)
        total = total + lax.dot_general(ones, rb_ref[...], NT, preferred_element_type=f32)
        ct_ref[...] = total[:1]

    @pl.when(j == 0)
    def _():
        block = pl.ds(pl.multiple_of(i * kb, kb), kb)
        for t, r_ref in enumerate((ra_ref, rb_ref)):
            cols = slice(t * h, (t + 1) * h)
            xv = xt_ref[:, cols]
            r = r_ref[block, :]
            for k in range(kb):
                wt_ref[k * q : (k + 1) * q, cols] = xv * r[k : k + 1, :]
            wt_ref[kb * q :, cols] = r

    for x_ref, at in ((xa_ref, 0), (xb_ref, 1)):

        @pl.when(j == at)
        def _():
            mine = pl.ds(pl.multiple_of(c * h, h), h)
            other = pl.ds(pl.multiple_of((1 - c) * h, h), h)
            rows = jnp.concatenate([x_ref[mine, :], x_ref[other, :]], axis=0)
            y = jnp.dot(wt_ref[...], rows, preferred_element_type=f32)
            o_ref[...] = y[: kb * q].reshape(kb, q, HALF)
            fm_ref[...] = y[kb * q :]


def sec(pos, ra, rb, xt, xa, xb, kb=16):
    k, _ = ra.shape
    n = xa.shape[0]
    q = xt.shape[0]
    whole = pl.BlockSpec(memory_space=pltpu.VMEM)
    spec = pltpu.PrefetchScalarGridSpec(
        num_scalar_prefetch=1,
        grid=(k // kb, 2),
        in_specs=[whole] * 5,
        out_specs=[
            pl.BlockSpec((kb, q, HALF), lambda i, j, p: (i, 0, p[0] + j * (1 - 2 * p[0]))),
            pl.BlockSpec((kb, HALF), lambda i, j, p: (i, p[0] + j * (1 - 2 * p[0]))),
            pl.BlockSpec((1, k), lambda i, j, p: (0, 0)),
        ],
        scratch_shapes=[pltpu.VMEM((kb * q + kb, n), bf16)],
    )
    return pl.pallas_call(
        functools.partial(sec_kernel, kb=kb),
        grid_spec=spec,
        out_shape=[
            jax.ShapeDtypeStruct((k, q, D), f32),
            jax.ShapeDtypeStruct((k, D), f32),
            jax.ShapeDtypeStruct((1, k), f32),
        ],
        compiler_params=pltpu.CompilerParams(vmem_limit_bytes=VMEM),
        cost_estimate=pl.CostEstimate(
            flops=2 * k * q * D * n, bytes_accessed=4 * k * q * D + 4 * n * D, transcendentals=0
        ),
        name="sec",
    )(pos, ra, rb, xt, xa, xb)


def swap(x, axis):
    return lax.ppermute(x, axis, [(0, 1), (1, 0)])


def layer(points, centres, whitening, log_prior):
    c, xl = lax.axis_index("c"), lax.axis_index("xl")
    pos = jnp.stack([c, xl, xl * 2 + c]).astype(jnp.int32)
    chips = lax.psum(1, CHIPS)
    groups = lax.psum(1, COMP)

    whitening = pltpu.with_memory_space_constraint(whitening, pltpu.HBM)
    rows = points.shape[0]
    own = lax.dynamic_slice(points, (0, c * HALF), (rows, HALF))
    away = swap(lax.dynamic_slice(points, (0, (1 - c) * HALF), (rows, HALF)), "c")
    pair = jnp.where(c == 0, jnp.concatenate([own, away]), jnp.concatenate([away, own]))
    pieces = jnp.broadcast_to(pair[None], (chips, 2 * rows, HALF))
    xa = lax.all_to_all(pieces, CHIPS, 0, 0, tiled=True)
    xa = xa.reshape(chips * 2 * rows, HALF)
    xb = swap(xa, "c")

    off, ld = prep(pos, whitening, centres)
    send, keep = dist(pos, whitening, off, ld, xa, xb)
    chip_part = keep + swap(send, "c")
    total = chip_part + swap(chip_part, "xl")
    xt = band(pos, xa, xb)

    logits = BETA * (log_prior[:, None] - total / D)
    peak = jnp.max(logits, axis=0)
    lse = peak + jnp.log(jnp.sum(jnp.exp(logits - peak[None, :]), axis=0))
    h = lse.shape[0]
    lanes = jnp.broadcast_to(lse.reshape(1, h // 128, 128), (groups, h // 128, 128))
    others = lax.all_to_all(lanes, COMP, 0, 0, tiled=True)
    top = jnp.max(others, axis=0)
    norm = (top + jnp.log(jnp.sum(jnp.exp(others - top[None]), axis=0))).reshape(h)
    ra = jnp.exp(logits - norm[None, :]).astype(bf16)
    rb = swap(ra, "c")
    second, first, counts = sec(pos, ra, rb, xt, xa, xb)
    return counts.reshape(-1), first, second


def solution(mesh):
    fine = Mesh(mesh.devices.reshape(2, 2, 2, 4, 4), ALL)
    band_axes = ("xl", "c")
    in_specs = (P(ALL, None), P(COMP, None), P(COMP, band_axes, None), P(COMP))
    out_specs = (P(COMP), P(COMP, None), P(COMP, band_axes, None))
    return jax.shard_map(layer, mesh=fine, in_specs=in_specs, out_specs=out_specs, check_vma=False)
```

time: 119 us -> 99 us (0.83)
  the two profiles are of different devices: /device:TPU:1 before, /device:TPU:0 now
where the time goes in v2:
time: 99 us; the launch traced here: 97.5 us
  Pallas kernels  42.4 us (43%)
  blocking collectives  41.5 us (42%)
  waiting for transfers between devices  9.96 us (10%)
  local copies, waits for them, and re-layouts  1.63 us (2%)
    all_to_all x1, blocking collectives, layer(): xa = lax.all_to_all(pieces, CHIPS, 0, 0, tiled=True)  27.7 us
    pallas_call x1, Pallas kernels, sec(): pl.pallas_call(functools.partial(sec_kernel, kb=kb), grid_spec=spec, out_...  17.3 us
    pallas_call x1, Pallas kernels, dist(): pl.pallas_call(functools.partial(dist_kernel, kb=kb, nt=nt), grid_spec=sp...  16.7 us
    all_to_all x1, blocking collectives, layer(): others = lax.all_to_all(lanes, COMP, 0, 0, tiled=True)  13.9 us
    ppermute x5, waiting for transfers between devices, swap(): return lax.ppermute(x, axis, [(0, 1), (1, 0)])  9.96 us
    pallas_call x1, Pallas kernels, prep(): pl.pallas_call(functools.partial(prep_kernel, kb=kb), grid_spec=spec, out...  7.74 us
  transfers between devices with their start and end apart: 5, of which 4 were waited for; matrix products, arithmetic and copies ran while one was open for 0% of the time, Pallas kernels for 9%

profile of v2, /device:TPU:0, one launch (start us, length us, event | category | flops | bytes accessed | tf_op | source)
XLA Modules:
  0.0 97.5 jit_solution(9820721536067896614)
XLA Ops:
  0.6 0.7 constant_dynamic-slice_fusion.1
  1.4 0.0 collective-permute-start
  1.4 1.2 %collective-permute-done = bf16[12,256]{1,0:T(8,128)(2,1)S(1)} collective-permute-done((bf16[12,256]{1,0:T(8,128)(2,1)S(1)}, bf16[12,256]{1,0:T(8,128)(2,1)S(1)}, u32[]{:S(2)}, u32[]{:S(2)}) %collective-permute-start) | collective-permute-done | bytes 6176 | tf_op jit(solution)/shard_map/ppermute | solution.py:206
  2.5 0.1 broadcast_in_dim.4
  2.6 27.7 %all_to_all.10 = bf16[64,24,256]{2,1,0:T(8,128)(2,1)S(1)} all-to-all(bf16[64,24,256]{2,1,0:T(8,128)(2,1)S(1)} %broadcast_in_dim.4), channel_id=1, replica_groups=mesh['xl'=2,'c'=2,'xh'=2,'y'=4,'z'=4] {'xl','xh','y','z'}, dimensions={0} | all-to-all | bytes 1572864 | tf_op jit(solution)/shard_map/all_to_all | solution.py:221
  30.3 0.0 collective-permute-start.1
  30.3 0.1 pad_add_fusion.pos
  30.3 0.0 copy-start
  30.3 0.8 copy-done
  31.2 7.7 %prep.1 = (f32[8,128,8]{2,1,0:T(8,128)S(1)}, f32[64,128]{1,0:T(8,128)S(1)}) custom-call(s32[3]{0:T(128)S(1)} %pad_add_fusion.pos, bf16[64,128,512]{2,1,0:T(8,128)(2,1)} %wb_ref.1, bf16[64,128,512]{2,1,0:T(8,128)(2,1)} %wb_ref.1, bf16[64,512]{1,0:T(8,128)(2,1)S(1)} %copy-done), custom_call_target="tpu_custom_call" | custom-call | flops 8000000 | bytes 10500000 | tf_op jit(solution)/shard_map/prep/pallas_call | solution.py:51
  38.9 0.0 collective-permute-done.1.xb_ref
  38.9 0.0 copy-start.1
  39.0 16.7 %dist.1 = (f32[64,768]{1,0:T(8,128)S(1)}, f32[64,768]{1,0:T(8,128)S(1)}) custom-call(s32[3]{0:T(128)S(1)} %pad_add_fusion.pos, bf16[64,128,512]{2,1,0:T(8,128)(2,1)} %wb_ref.1, bf16[64,128,512]{2,1,0:T(8,128)(2,1)} %wb_ref.1, f32[8,128,8]{2,1,0:T(8,128)S(1)} %get-tuple-element.10.off_ref, f32[64,128]{1,0:T(8,128)S(1)} %get-tuple-element.11.ld_ref, ...), custom_call_target="tpu_custom_call" | custom-call | flops 12884901888 | bytes 10354688 | tf_op jit(solution)/shard_map/dist/pallas_call | solution.py:98
  55.7 0.6 collective-permute-start.2
  56.3 1.1 %collective-permute-done.2 = f32[64,768]{1,0:T(8,128)S(1)} collective-permute-done((f32[64,768]{1,0:T(8,128)S(1)}, f32[64,768]{1,0:T(8,128)S(1)}, u32[]{:S(2)}, u32[]{:S(2)}) %collective-permute-start.2) | collective-permute-done | bytes 196640 | tf_op jit(solution)/shard_map/ppermute | solution.py:206
  57.4 0.1 collective-permute-start.3
  57.5 7.2 %collective-permute-done.3 = f32[64,768]{1,0:T(8,128)S(1)} collective-permute-done((f32[64,768]{1,0:T(8,128)S(1)}, f32[64,768]{1,0:T(8,128)S(1)}, u32[]{:S(2)}, u32[]{:S(2)}) %collective-permute-start.3) | collective-permute-done | bytes 196640 | tf_op jit(solution)/shard_map/ppermute | solution.py:206
  64.7 0.0 copy-done.1
  64.7 0.1 fusion
  64.9 13.9 %all_to_all.11 = f32[32,6,128]{2,1,0:T(8,128)S(1)} all-to-all(f32[32,6,128]{2,1,0:T(8,128)S(1)} %broadcast_in_dim.5), channel_id=1, replica_groups=mesh['xl'=2,'c'=2,'xh'=2,'y'=4,'z'=4] {'xh','y','z'}, dimensions={0} | all-to-all | bytes 196608 | tf_op jit(solution)/shard_map/all_to_all | solution.py:236
  78.9 0.1 collective-permute-start.4
  79.0 0.7 band.1.xt_ref
  79.7 0.6 collective-permute-done.4.rb_ref
  80.3 17.3 %sec.1 = (f32[64,128,512]{2,1,0:T(8,128)}, f32[64,512]{1,0:T(8,128)}, f32[1,64]{1,0:T(1,128)}) custom-call(s32[3]{0:T(128)S(1)} %pad_add_fusion.pos, bf16[64,768]{1,0:T(8,128)(2,1)S(1)} %exponential_convert_fusion.ra_ref, bf16[64,768]{1,0:T(8,128)(2,1)S(1)} %collective-permute-done.4.rb_ref, bf16[128,1536]{1,0:T(8,128)(2,1)S(1)} %band.1.xt_ref, ...), custom_call_target="tpu_custom_call" | custom-call | flops 12884901888 | bytes 19922944 | tf_op jit(solution)/shard_map/sec/pallas_call | solution.py:189
  (9 shorter events, 0.2 us)
Async XLA Ops:
  1.4 1.2 %collective-permute-start = (bf16[12,256]{1,0:T(8,128)(2,1)S(1)}, bf16[12,256]{1,0:T(8,128)(2,1)S(1)}, u32[]{:S(2)}, u32[]{:S(2)}) collective-permute-start(bf16[12,256]{1,0:T(8,128)(2,1)S(1)} %get-tuple-element.20), channel_id=1, source_target_pairs={{0,32},{32,0},{1,33},{33,1},{2,34},{34,2},{3,35},{35,3},{4,36},{36... | collective-permute-start | bytes 18440 | tf_op jit(solution)/shard_map/ppermute | solution.py:206
  30.3 8.7 %collective-permute-start.1 = (bf16[1536,256]{1,0:T(8,128)(2,1)S(1)}, bf16[1536,256]{1,0:T(8,128)(2,1)S(1)}, u32[]{:S(2)}, u32[]{:S(2)}) collective-permute-start(bf16[1536,256]{1,0:T(8,128)(2,1)S(1)} %bitcast.9), channel_id=1, source_target_pairs={{0,32},{32,0},{1,33},{33,1},{2,34},{34,2},{3,35},{35,3},{4,36},{36... | collective-permute-start | bytes 2359304 | tf_op jit(solution)/shard_map/ppermute | solution.py:206
  30.3 0.8 copy-start
  38.9 25.7 %copy-start.1 = (f32[64]{0:T(128)S(1)}, f32[64]{0:T(128)}, u32[]{:S(2)}) copy-start(f32[64]{0:T(128)} %param.7) | copy-start | bytes 772
  55.7 1.7 %collective-permute-start.2 = (f32[64,768]{1,0:T(8,128)S(1)}, f32[64,768]{1,0:T(8,128)S(1)}, u32[]{:S(2)}, u32[]{:S(2)}) collective-permute-start(f32[64,768]{1,0:T(8,128)S(1)} %get-tuple-element.13), channel_id=1, source_target_pairs={{0,32},{32,0},{1,33},{33,1},{2,34},{34,2},{3,35},{35,3},{4,36},{36... | collective-permute-start | bytes 589832 | tf_op jit(solution)/shard_map/ppermute | solution.py:206
  57.4 7.3 %collective-permute-start.3 = (f32[64,768]{1,0:T(8,128)S(1)}, f32[64,768]{1,0:T(8,128)S(1)}, u32[]{:S(2)}, u32[]{:S(2)}) collective-permute-start(f32[64,768]{1,0:T(8,128)S(1)} %add.38), channel_id=1, source_target_pairs={{0,64},{64,0},{1,65},{65,1},{2,66},{66,2},{3,67},{67,3},{4,68},{68... | collective-permute-start | bytes 589832 | tf_op jit(solution)/shard_map/ppermute | solution.py:206
  78.9 1.4 %collective-permute-start.4 = (bf16[64,768]{1,0:T(8,128)(2,1)S(1)}, bf16[64,768]{1,0:T(8,128)(2,1)S(1)}, u32[]{:S(2)}, u32[]{:S(2)}) collective-permute-start(bf16[64,768]{1,0:T(8,128)(2,1)S(1)} %exponential_convert_fusion.ra_ref), channel_id=1, source_target_pairs={{0,32},{32,0},{1,33},{33,1},{2,34},{34,2},{3,35},{35,3},{4,36},{36... | collective-permute-start | bytes 294920 | tf_op jit(solution)/shard_map/ppermute | solution.py:206

commit v3 on v2

v3 whole, which is shorter than its diff:
```python
import functools

import jax
import jax.numpy as jnp
from jax import lax
from jax.experimental import pallas as pl
from jax.experimental.pallas import tpu as pltpu
from jax.sharding import Mesh, PartitionSpec as P

D = 512
HALF = D // 2
BETA = 1.25
NT = (((1,), (1,)), ((), ()))
VMEM = 24 << 20
KB_DIST = 16
f32 = jnp.float32
bf16 = jnp.bfloat16
ALL = ("xl", "c", "xh", "y", "z")
CHIPS = ("xl", "xh", "y", "z")
COMP = ("xh", "y", "z")


def prep_kernel(pos, w_ref, wd_ref, c_ref, off_ref, ld_ref, *, kb):
    q = w_ref.shape[1]
    row = lax.broadcasted_iota(jnp.int32, (q, q), 0)
    eye = row == lax.broadcasted_iota(jnp.int32, (q, q), 1)
    for k in range(kb):
        prod = w_ref[k].astype(f32) * c_ref[k : k + 1, :].astype(f32)
        off_ref[0, :, k : k + 1] = jnp.sum(prod, axis=1, keepdims=True)
        diag = jnp.sum(jnp.where(eye, wd_ref[k].astype(f32), 0.0), axis=0, keepdims=True)
        total = jnp.sum(jnp.log(diag), axis=1, keepdims=True)
        ld_ref[k : k + 1, :] = jnp.broadcast_to(total, (1, 128))


def prep(pos, w, cen, kb=8):
    k, q, _ = w.shape
    spec = pltpu.PrefetchScalarGridSpec(
        num_scalar_prefetch=1,
        grid=(k // kb,),
        in_specs=[
            pl.BlockSpec((kb, q, D), lambda i, p: (i, 0, 0)),
            pl.BlockSpec((kb, q, q), lambda i, p: (i, 0, p[0])),
            pl.BlockSpec((kb, D), lambda i, p: (i, 0)),
        ],
        out_specs=[
            pl.BlockSpec((1, q, kb), lambda i, p: (i, 0, 0)),
            pl.BlockSpec((kb, 128), lambda i, p: (i, 0)),
        ],
    )
    return pl.pallas_call(
        functools.partial(prep_kernel, kb=kb),
        grid_spec=spec,
        out_shape=[
            jax.ShapeDtypeStruct((k // kb, q, kb), f32),
            jax.ShapeDtypeStruct((k, 128), f32),
        ],
        compiler_params=pltpu.CompilerParams(vmem_limit_bytes=VMEM),
        cost_estimate=pl.CostEstimate(flops=8_000_000, bytes_accessed=10_500_000, transcendentals=8192),
        name="prep",
    )(pos, w, w, cen)


def dist_kernel(w_ref, off_ref, ld_ref, x_ref, o_ref, *, kb, nt):
    q = w_ref.shape[1]
    n = o_ref.shape[1]
    w = w_ref[...].reshape(kb * q, D)
    for t in range(n // nt):
        y = lax.dot_general(w, x_ref[t * nt : (t + 1) * nt, :], NT, preferred_element_type=f32)
        for k in range(kb):
            u = y[k * q : (k + 1) * q] - off_ref[k // 8, :, k % 8 : k % 8 + 1]
            part = 0.5 * jnp.sum(u * u, axis=0, keepdims=True) - ld_ref[k : k + 1, :1]
            o_ref[k : k + 1, t * nt : (t + 1) * nt] = part


def dist(w, off, ld, x, kb=KB_DIST, nt=256):
    k, q, _ = w.shape
    n = x.shape[0]
    return pl.pallas_call(
        functools.partial(dist_kernel, kb=kb, nt=nt),
        grid=(k // kb,),
        in_specs=[
            pl.BlockSpec((kb, q, D), lambda i: (i, 0, 0)),
            pl.BlockSpec((kb // 8, q, 8), lambda i: (i, 0, 0)),
            pl.BlockSpec((kb, 128), lambda i: (i, 0)),
            pl.BlockSpec(memory_space=pltpu.VMEM),
        ],
        out_specs=pl.BlockSpec((kb, n), lambda i: (i, 0)),
        out_shape=jax.ShapeDtypeStruct((k, n), f32),
        compiler_params=pltpu.CompilerParams(vmem_limit_bytes=VMEM),
        cost_estimate=pl.CostEstimate(
            flops=2 * k * q * D * n, bytes_accessed=2 * k * q * D + 2 * n * D + 4 * k * n, transcendentals=0
        ),
        name="dist",
    )(w, off, ld, x)


def band_kernel(pos, xa_ref, xb_ref, o_ref):
    h = xa_ref.shape[0]
    cols = pl.ds(pl.multiple_of(pos[0] * 128, 128), 128)
    for t, x_ref in enumerate((xa_ref, xb_ref)):
        o_ref[:, t * h : (t + 1) * h] = x_ref[:, cols].astype(f32).T.astype(bf16)


def band(pos, xa, xb):
    h = xa.shape[0]
    whole = pl.BlockSpec(memory_space=pltpu.VMEM)
    spec = pltpu.PrefetchScalarGridSpec(num_scalar_prefetch=1, grid=(1,), in_specs=[whole] * 2, out_specs=whole)
    return pl.pallas_call(
        band_kernel,
        grid_spec=spec,
        out_shape=jax.ShapeDtypeStruct((128, 2 * h), bf16),
        compiler_params=pltpu.CompilerParams(vmem_limit_bytes=8 << 20),
        cost_estimate=pl.CostEstimate(flops=0, bytes_accessed=2_000_000, transcendentals=0),
        name="band",
    )(pos, xa, xb)


def sec_kernel(ra_ref, rb_ref, xt_ref, xa_ref, xb_ref, o_ref, fm_ref, ct_ref, wt_ref, *, kb):
    q = xt_ref.shape[0]
    h = ra_ref.shape[1]
    i, j = pl.program_id(0), pl.program_id(1)

    @pl.when((i == 0) & (j == 0))
    def _():
        ones = jnp.ones((8, h), bf16)
        total = lax.dot_general(ones, ra_ref[...], NT, preferred_element_type=f32)
        total = total + lax.dot_general(ones, rb_ref[...], NT, preferred_element_type=f32)
        ct_ref[...] = total[:1]

    @pl.when(j == 0)
    def _():
        block = pl.ds(pl.multiple_of(i * kb, kb), kb)
        for t, r_ref in enumerate((ra_ref, rb_ref)):
            cols = slice(t * h, (t + 1) * h)
            xv = xt_ref[:, cols]
            r = r_ref[block, :]
            for k in range(kb):
                wt_ref[k * q : (k + 1) * q, cols] = xv * r[k : k + 1, :]
            wt_ref[kb * q :, cols] = r

    for half in range(2):

        @pl.when(j == half)
        def _():
            cols = slice(half * HALF, (half + 1) * HALF)
            rows = jnp.concatenate([xa_ref[:, cols], xb_ref[:, cols]], axis=0)
            y = jnp.dot(wt_ref[...], rows, preferred_element_type=f32)
            o_ref[...] = y[: kb * q].reshape(kb, q, HALF)
            fm_ref[...] = y[kb * q :]


def sec(ra, rb, xt, xa, xb, kb=16):
    k, _ = ra.shape
    q, n = xt.shape
    whole = pl.BlockSpec(memory_space=pltpu.VMEM)
    return pl.pallas_call(
        functools.partial(sec_kernel, kb=kb),
        grid=(k // kb, 2),
        in_specs=[whole] * 5,
        out_specs=[
            pl.BlockSpec((kb, q, HALF), lambda i, j: (i, 0, j)),
            pl.BlockSpec((kb, HALF), lambda i, j: (i, j)),
            pl.BlockSpec((1, k), lambda i, j: (0, 0)),
        ],
        out_shape=[
            jax.ShapeDtypeStruct((k, q, D), f32),
            jax.ShapeDtypeStruct((k, D), f32),
            jax.ShapeDtypeStruct((1, k), f32),
        ],
        scratch_shapes=[pltpu.VMEM((kb * q + kb, n), bf16)],
        compiler_params=pltpu.CompilerParams(vmem_limit_bytes=VMEM),
        cost_estimate=pl.CostEstimate(
            flops=2 * k * q * D * n, bytes_accessed=4 * k * q * D + 2 * n * D, transcendentals=0
        ),
        name="sec",
    )(ra, rb, xt, xa, xb)


def swap(x, axis):
    return lax.ppermute(x, axis, [(0, 1), (1, 0)])


def log_sum(values):
    peak = jnp.max(values, axis=0)
    return peak + jnp.log(jnp.sum(jnp.exp(values - peak[None]), axis=0))


def layer(points, centres, whitening, log_prior):
    pos = (lax.axis_index("xl") * 2 + lax.axis_index("c")).astype(jnp.int32).reshape(1)
    chips = lax.psum(1, CHIPS)
    groups = lax.psum(1, COMP)
    whitening = pltpu.with_memory_space_constraint(whitening, pltpu.HBM)

    m = points.size // 128
    pieces = jnp.broadcast_to(points.reshape(1, m, 128), (chips, m, 128))
    xa = lax.all_to_all(pieces, CHIPS, 0, 0, tiled=True)
    xa = xa.reshape(chips * points.shape[0], D)
    xb = swap(xa, "c")

    off, ld = prep(pos, whitening, centres)
    send = dist(whitening, off, ld, xa)
    got = swap(send, "c")
    keep = dist(whitening, off, ld, xb)
    chip_part = keep + got
    total_b = chip_part + swap(chip_part, "xl")
    total_a = swap(total_b, "c")
    xt = band(pos, xa, xb)

    logits_a = BETA * (log_prior[:, None] - total_a / D)
    logits_b = BETA * (log_prior[:, None] - total_b / D)
    h = logits_a.shape[1]
    lse = jnp.concatenate([log_sum(logits_a), log_sum(logits_b)])
    lanes = jnp.broadcast_to(lse.reshape(1, 1, 2 * h), (groups, 1, 2 * h))
    others = lax.all_to_all(lanes, COMP, 0, 0, tiled=True)
    norm = log_sum(others.reshape(groups, 2 * h))
    ra = jnp.exp(logits_a - norm[None, :h]).astype(bf16)
    rb = jnp.exp(logits_b - norm[None, h:]).astype(bf16)
    second, first, counts = sec(ra, rb, xt, xa, xb)
    return counts.reshape(-1), first, second


def solution(mesh):
    fine = Mesh(mesh.devices.reshape(2, 2, 2, 4, 4), ALL)
    band_axes = ("xl", "c")
    in_specs = (P(ALL, None), P(COMP, None), P(COMP, band_axes, None), P(COMP))
    out_specs = (P(COMP), P(COMP, None), P(COMP, band_axes, None))
    return jax.shard_map(layer, mesh=fine, in_specs=in_specs, out_specs=out_specs, check_vma=False)
```

time: 99 us -> 97.9 us (0.989); the launches traced: 97.5 us -> 97.4 us
  blocking collectives: 41.5 us -> 27.3 us
  waiting for transfers between devices: 9.96 us -> 18.5 us
  starting transfers between devices: 0.81 us -> 4.91 us
  local copies, waits for them, and re-layouts: 1.63 us -> 2.93 us
    all_to_all x1 -> x0, blocking collectives: 13.9 us -> none  [layer(): others = lax.all_to_all(lanes, COMP, 0, 0, tiled=True)]
    all_to_all x0 -> x1, waiting for transfers between devices: none -> 10.2 us  [layer(): others = lax.all_to_all(lanes, COMP, 0, 0, tiled=True)]
    all_to_all x0 -> x1, starting transfers between devices: none -> 4 us  [layer(): others = lax.all_to_all(lanes, COMP, 0, 0, tiled=True)]
    ppermute x5 -> x4, waiting for transfers between devices: 9.96 us -> 8.28 us  [swap(): return lax.ppermute(x, axis, [(0, 1), (1, 0)])]
    broadcast_in_dim x2 -> x3, local copies, waits for them, and re-layouts: 0.06 us -> 1.62 us  [the longest x2 0.84 us: layer(): pieces = jnp.broadcast_to(points.reshape(1, m, 128), (chips, m, 128))]
    pallas_call x2 -> x3, Pallas kernels: 34 us -> 34.9 us  [the longest x2 18.4 us: dist(): pl.pallas_call(functools.partial(dist_kernel, kb=kb, nt=nt), grid=(k // k...]
  transfers between devices with their start and end apart: 5 -> 5, of which waited for: 4 -> 3; matrix products, arithmetic and copies ran while one was open for 0% -> 0% of each run, Pallas kernels for 9% -> 26%
where the time goes in v3:
time: 97.9 us; the launch traced here: 97.4 us
  Pallas kernels  42.2 us (43%)
  blocking collectives  27.3 us (28%)
  waiting for transfers between devices  18.5 us (19%)
  starting transfers between devices  4.91 us (5%)
  local copies, waits for them, and re-layouts  2.93 us (3%)
    all_to_all x1, blocking collectives, layer(): xa = lax.all_to_all(pieces, CHIPS, 0, 0, tiled=True)  27.3 us
    pallas_call x2, Pallas kernels, dist(): pl.pallas_call(functools.partial(dist_kernel, kb=kb, nt=nt), grid=(k // k...  18.4 us
    pallas_call x1, Pallas kernels, sec(): pl.pallas_call(functools.partial(sec_kernel, kb=kb), grid=(k // kb, 2), i...  16.5 us
    all_to_all x1, waiting for transfers between devices, layer(): others = lax.all_to_all(lanes, COMP, 0, 0, tiled=True)  10.2 us
    ppermute x4, waiting for transfers between devices, swap(): return lax.ppermute(x, axis, [(0, 1), (1, 0)])  8.28 us
    pallas_call x1, Pallas kernels, prep(): pl.pallas_call(functools.partial(prep_kernel, kb=kb), grid_spec=spec, out...  7.19 us
    all_to_all x1, starting transfers between devices, layer(): others = lax.all_to_all(lanes, COMP, 0, 0, tiled=True)  4 us
  transfers between devices with their start and end apart: 5, of which 3 were waited for; matrix products, arithmetic and copies ran while one was open for 0% of the time, Pallas kernels for 26%

profile of v3, /device:TPU:0, one launch (start us, length us, event | category | flops | bytes accessed | tf_op | source)
XLA Modules:
  0.0 97.4 jit_solution(13329583461624215086)
XLA Ops:
  0.6 0.7 broadcast_in_dim.6
  1.4 0.1 broadcast_in_dim.7
  1.5 27.3 %all_to_all.10 = bf16[64,48,128]{2,1,0:T(8,128)(2,1)S(1)} all-to-all(bf16[64,48,128]{2,1,0:T(8,128)(2,1)S(1)} %broadcast_in_dim.7), channel_id=1, replica_groups=mesh['xl'=2,'c'=2,'xh'=2,'y'=4,'z'=4] {'xl','xh','y','z'}, dimensions={0} | all-to-all | bytes 1572864 | tf_op jit(solution)/shard_map/all_to_all | solution.py:196
  28.8 0.5 reshape.31.x_ref.xa_ref
  29.3 0.1 collective-permute-start
  29.4 0.0 copy-start
  29.4 0.8 copy-done
  30.2 7.2 %prep.1 = (f32[8,128,8]{2,1,0:T(8,128)S(1)}, f32[64,128]{1,0:T(8,128)S(1)}) custom-call(s32[1]{0:T(128)} %bitcast.pos, bf16[64,128,512]{2,1,0:T(8,128)(2,1)} %w_ref.5, bf16[64,128,512]{2,1,0:T(8,128)(2,1)} %w_ref.5, bf16[64,512]{1,0:T(8,128)(2,1)S(1)} %copy-done), custom_call_target="tpu_custom_call" | custom-call | flops 8000000 | bytes 10500000 | tf_op jit(solution)/shard_map/prep/pallas_call | solution.py:50
  37.4 9.2 %dist.3 = f32[64,768]{1,0:T(8,128)S(1)} custom-call(bf16[64,128,512]{2,1,0:T(8,128)(2,1)} %w_ref.5, f32[8,128,8]{2,1,0:T(8,128)S(1)} %get-tuple-element.8.off_ref, f32[64,128]{1,0:T(8,128)S(1)} %get-tuple-element.9.ld_ref, bf16[768,512]{1,0:T(8,128)(2,1)S(1)} %reshape.31.x_ref.xa_ref), custom_call_target="tpu_custom_call" | custom-call | flops 6442450944 | bytes 9371648 | tf_op jit(solution)/shard_map/dist/pallas_call | solution.py:78
  46.6 0.0 copy-start.1
  46.6 0.7 collective-permute-start.1
  47.3 0.0 collective-permute-done.x_ref.xb_ref
  47.3 9.2 %dist.2 = f32[64,768]{1,0:T(8,128)S(1)} custom-call(bf16[64,128,512]{2,1,0:T(8,128)(2,1)} %w_ref.5, f32[8,128,8]{2,1,0:T(8,128)S(1)} %get-tuple-element.8.off_ref, f32[64,128]{1,0:T(8,128)S(1)} %get-tuple-element.9.ld_ref, bf16[768,512]{1,0:T(8,128)(2,1)S(1)} %collective-permute-done.x_ref.xb_ref), custom_call_target="tpu_custom_call" | custom-call | flops 6442450944 | bytes 9371648 | tf_op jit(solution)/shard_map/dist/pallas_call | solution.py:78
  56.5 0.0 collective-permute-done.1
  56.6 0.1 collective-permute-start.2
  56.7 6.8 %collective-permute-done.2 = f32[64,768]{1,0:T(8,128)S(1)} collective-permute-done((f32[64,768]{1,0:T(8,128)S(1)}, f32[64,768]{1,0:T(8,128)S(1)}, u32[]{:S(2)}, u32[]{:S(2)}) %collective-permute-start.2) | collective-permute-done | bytes 196640 | tf_op jit(solution)/shard_map/ppermute | solution.py:180
  63.5 0.1 collective-permute-start.3
  63.6 1.4 %collective-permute-done.3 = f32[64,768]{1,0:T(8,128)S(1)} collective-permute-done((f32[64,768]{1,0:T(8,128)S(1)}, f32[64,768]{1,0:T(8,128)S(1)}, u32[]{:S(2)}, u32[]{:S(2)}) %collective-permute-start.3) | collective-permute-done | bytes 196640 | tf_op jit(solution)/shard_map/ppermute | solution.py:180
  65.1 0.0 copy-done.1
  65.1 0.1 fusion.2
  65.2 0.1 exponential_reduce_fusion.1
  65.3 0.1 exponential_reduce_fusion
  65.5 0.8 broadcast_in_dim.8
  66.2 4.0 %all-to-all-start.1 = ((f32[32,1,1536]{2,1,0:T(1,128)}), f32[32,1,1536]{2,1,0:T(1,128)S(1)}, u32[]{:S(2)}, u32[]{:S(2)}) async-start(f32[32,1,1536]{2,1,0:T(1,128)} %broadcast_in_dim.8), calls=%async_computation.1 | async-start | bytes 393216 | tf_op jit(solution)/shard_map/all_to_all | solution.py:214
  70.2 0.2 band.1.xt_ref
  70.4 10.2 %all-to-all-done.1 = f32[32,1,1536]{2,1,0:T(1,128)S(1)} async-done(((f32[32,1,1536]{2,1,0:T(1,128)}), f32[32,1,1536]{2,1,0:T(1,128)S(1)}, u32[]{:S(2)}, u32[]{:S(2)}) %all-to-all-start.1) | async-done | bytes 196640 | tf_op jit(solution)/shard_map/all_to_all | solution.py:214
  80.6 0.1 reduce_max.29
  80.8 0.2 exponential_convert_fusion
  81.0 16.5 %sec.1 = (f32[64,128,512]{2,1,0:T(8,128)}, f32[64,512]{1,0:T(8,128)}, f32[1,64]{1,0:T(1,128)}) custom-call(bf16[64,768]{1,0:T(8,128)(2,1)S(1)} %get-tuple-element.18.ra_ref, bf16[64,768]{1,0:T(8,128)(2,1)S(1)} %get-tuple-element.17.rb_ref, bf16[128,1536]{1,0:T(8,128)(2,1)S(1)} %band.1.xt_ref, bf16[768,512]{1,0:T(8,128)(2,1)S(1)} %reshape.31.x_ref.xa_ref, ...), custom_call_target="tpu_custom_call" | custom-call | flops 12884901888 | bytes 18350080 | tf_op jit(solution)/shard_map/sec/pallas_call | solution.py:156
  (7 shorter events, 0.1 us)
Async XLA Ops:
  29.3 18.0 %collective-permute-start = (bf16[768,512]{1,0:T(8,128)(2,1)S(1)}, bf16[768,512]{1,0:T(8,128)(2,1)S(1)}, u32[]{:S(2)}, u32[]{:S(2)}) collective-permute-start(bf16[768,512]{1,0:T(8,128)(2,1)S(1)} %reshape.31.x_ref.xa_ref), channel_id=1, source_target_pairs={{0,32},{32,0},{1,33},{33,1},{2,34},{34,2},{3,35},{35,3},{4,36},{36... | collective-permute-start | bytes 2359304 | tf_op jit(solution)/shard_map/ppermute | solution.py:180
  29.4 0.8 copy-start
  46.6 18.4 %copy-start.1 = (f32[64]{0:T(128)S(1)}, f32[64]{0:T(128)}, u32[]{:S(2)}) copy-start(f32[64]{0:T(128)} %param.7) | copy-start | bytes 772
  46.6 9.9 %collective-permute-start.1 = (f32[64,768]{1,0:T(8,128)S(1)}, f32[64,768]{1,0:T(8,128)S(1)}, u32[]{:S(2)}, u32[]{:S(2)}) collective-permute-start(f32[64,768]{1,0:T(8,128)S(1)} %dist.3), channel_id=1, source_target_pairs={{0,32},{32,0},{1,33},{33,1},{2,34},{34,2},{3,35},{35,3},{4,36},{36... | collective-permute-start | bytes 589832 | tf_op jit(solution)/shard_map/ppermute | solution.py:180
  56.6 6.9 %collective-permute-start.2 = (f32[64,768]{1,0:T(8,128)S(1)}, f32[64,768]{1,0:T(8,128)S(1)}, u32[]{:S(2)}, u32[]{:S(2)}) collective-permute-start(f32[64,768]{1,0:T(8,128)S(1)} %add.19), channel_id=1, source_target_pairs={{0,64},{64,0},{1,65},{65,1},{2,66},{66,2},{3,67},{67,3},{4,68},{68... | collective-permute-start | bytes 589832 | tf_op jit(solution)/shard_map/ppermute | solution.py:180
  63.5 1.5 %collective-permute-start.3 = (f32[64,768]{1,0:T(8,128)S(1)}, f32[64,768]{1,0:T(8,128)S(1)}, u32[]{:S(2)}, u32[]{:S(2)}) collective-permute-start(f32[64,768]{1,0:T(8,128)S(1)} %add.20), channel_id=1, source_target_pairs={{0,32},{32,0},{1,33},{33,1},{2,34},{34,2},{3,35},{35,3},{4,36},{36... | collective-permute-start | bytes 589832 | tf_op jit(solution)/shard_map/ppermute | solution.py:180
  66.2 14.4 %all-to-all-start.1 = ((f32[32,1,1536]{2,1,0:T(1,128)}), f32[32,1,1536]{2,1,0:T(1,128)S(1)}, u32[]{:S(2)}, u32[]{:S(2)}) async-start(f32[32,1,1536]{2,1,0:T(1,128)} %broadcast_in_dim.8), calls=%async_computation.1 | async-start | bytes 393216 | tf_op jit(solution)/shard_map/all_to_all | solution.py:214

commit v4 on v3

--- a/solution.py
+++ b/solution.py
@@ -60,38 +60,89 @@
     )(pos, w, w, cen)
 
 
-def dist_kernel(w_ref, off_ref, ld_ref, x_ref, o_ref, *, kb, nt):
+def dist_block(w_ref, off_ref, ld_ref, x_ref, o_ref, i, kb, nt, start):
     q = w_ref.shape[1]
     n = o_ref.shape[1]
-    w = w_ref[...].reshape(kb * q, D)
+    block = pl.ds(pl.multiple_of(i * kb, kb), kb)
+    w = w_ref[block].reshape(kb * q, D)
+    ld = ld_ref[block, :]
     for t in range(n // nt):
-        y = lax.dot_general(w, x_ref[t * nt : (t + 1) * nt, :], NT, preferred_element_type=f32)
+        rows = slice(start + t * nt, start + (t + 1) * nt)
+        y = lax.dot_general(w, x_ref[rows, :], NT, preferred_element_type=f32)
+        parts = []
         for k in range(kb):
-            u = y[k * q : (k + 1) * q] - off_ref[k // 8, :, k % 8 : k % 8 + 1]
-            part = 0.5 * jnp.sum(u * u, axis=0, keepdims=True) - ld_ref[k : k + 1, :1]
-            o_ref[k : k + 1, t * nt : (t + 1) * nt] = part
-
-
-def dist(w, off, ld, x, kb=KB_DIST, nt=256):
+            u = y[k * q : (k + 1) * q] - off_ref[i * (kb // 8) + k // 8, :, k % 8 : k % 8 + 1]
+            parts.append(0.5 * jnp.sum(u * u, axis=0, keepdims=True) - ld[k : k + 1, :1])
+        o_ref[block, t * nt : (t + 1) * nt] = jnp.concatenate(parts, axis=0)
+
+
+def first_kernel(w_hbm, off_ref, ld_ref, x_ref, o_ref, w_ref, sem, *, kb, nt):
+    count = w_ref.shape[0]
+
+    def copy(i):
+        block = pl.ds(i * 8, 8)
+        return pltpu.make_async_copy(w_hbm.at[block], w_ref.at[block], sem.at[i])
+
+    for i in range(count // 8):
+        copy(i).start()
+
+    @pl.loop(0, count // kb)
+    def _(i):
+        for j in range(kb // 8):
+            copy(i * (kb // 8) + j).wait()
+        dist_block(w_ref, off_ref, ld_ref, x_ref, o_ref, i, kb, nt, 0)
+
+
+def dist_kernel(w_ref, off_ref, ld_ref, x_ref, o_ref, *, kb, nt, start):
+    @pl.loop(0, w_ref.shape[0] // kb)
+    def _(i):
+        dist_block(w_ref, off_ref, ld_ref, x_ref, o_ref, i, kb, nt, start)
+
+
+def dist(w, off, ld, x, start, n, first=False, kb=KB_DIST, nt=256):
     k, q, _ = w.shape
-    n = x.shape[0]
-    return pl.pallas_call(
-        functools.partial(dist_kernel, kb=kb, nt=nt),
-        grid=(k // kb,),
-        in_specs=[
-            pl.BlockSpec((kb, q, D), lambda i: (i, 0, 0)),
-            pl.BlockSpec((kb // 8, q, 8), lambda i: (i, 0, 0)),
-            pl.BlockSpec((kb, 128), lambda i: (i, 0)),
-            pl.BlockSpec(memory_space=pltpu.VMEM),
-        ],
-        out_specs=pl.BlockSpec((kb, n), lambda i: (i, 0)),
-        out_shape=jax.ShapeDtypeStruct((k, n), f32),
+    whole = pl.BlockSpec(memory_space=pltpu.VMEM)
+    if first:
+        kernel = functools.partial(first_kernel, kb=kb, nt=nt)
+    else:
+        kernel = functools.partial(dist_kernel, kb=kb, nt=nt, start=start)
+    out = jax.ShapeDtypeStruct((k, n), f32)
+    return pl.pallas_call(
+        kernel,
+        in_specs=[pl.BlockSpec(memory_space=pl.ANY) if first else whole] + [whole] * 3,
+        out_specs=[whole, whole] if first else whole,
+        out_shape=[out, jax.ShapeDtypeStruct(w.shape, bf16)] if first else out,
+        scratch_shapes=[pltpu.SemaphoreType.DMA((k // 8,))] if first else [],
         compiler_params=pltpu.CompilerParams(vmem_limit_bytes=VMEM),
         cost_estimate=pl.CostEstimate(
             flops=2 * k * q * D * n, bytes_accessed=2 * k * q * D + 2 * n * D + 4 * k * n, transcendentals=0
         ),
-        name="dist",
+        name="dist_first" if first else "dist",
     )(w, off, ld, x)
+
+
+def rows_kernel(g_ref, o_ref, wide_ref):
+    count, m, _ = g_ref.shape
+    wide_ref[...] = g_ref[...].astype(f32).reshape(count * m, 128)
+    n = o_ref.shape[0]
+    parts = D // 128
+    for b in range(parts):
+        o_ref[:, b * 128 : (b + 1) * 128] = wide_ref[pl.ds(b, n, stride=parts), :].astype(bf16)
+
+
+def to_rows(g):
+    count, m, _ = g.shape
+    whole = pl.BlockSpec(memory_space=pltpu.VMEM)
+    return pl.pallas_call(
+        rows_kernel,
+        in_specs=[whole],
+        out_specs=whole,
+        out_shape=jax.ShapeDtypeStruct((count * m * 128 // D, D), bf16),
+        scratch_shapes=[pltpu.VMEM((count * m, 128), f32)],
+        compiler_params=pltpu.CompilerParams(vmem_limit_bytes=8 << 20),
+        cost_estimate=pl.CostEstimate(flops=0, bytes_accessed=2_000_000, transcendentals=0),
+        name="rows",
+    )(g)
 
 
 def band_kernel(pos, xa_ref, xb_ref, o_ref):
@@ -180,6 +231,10 @@
     return lax.ppermute(x, axis, [(0, 1), (1, 0)])
 
 
+def after(x, y):
+    return lax.optimization_barrier((x, y))[0]
+
+
 def log_sum(values):
     peak = jnp.max(values, axis=0)
     return peak + jnp.log(jnp.sum(jnp.exp(values - peak[None]), axis=0))
@@ -194,21 +249,26 @@
     m = points.size // 128
     pieces = jnp.broadcast_to(points.reshape(1, m, 128), (chips, m, 128))
     xa = lax.all_to_all(pieces, CHIPS, 0, 0, tiled=True)
-    xa = xa.reshape(chips * points.shape[0], D)
-    xb = swap(xa, "c")
-
+    xa = to_rows(xa)
     off, ld = prep(pos, whitening, centres)
-    send = dist(whitening, off, ld, xa)
-    got = swap(send, "c")
-    keep = dist(whitening, off, ld, xb)
-    chip_part = keep + got
-    total_b = chip_part + swap(chip_part, "xl")
+    h = xa.shape[0]
+    cut = 2 * h // 3
+    send1, w = dist(whitening, off, ld, xa, 0, cut, first=True)
+    xb = swap(after(xa, send1), "c")
+    send2 = dist(w, off, ld, xa, cut, h - cut)
+    got1 = swap(after(send1, send2), "c")
+    got2 = swap(send2, "c")
+    chip1 = dist(w, off, ld, xb, 0, cut) + got1
+    far1 = swap(chip1, "xl")
+    keep2 = dist(w, off, ld, xb, cut, h - cut)
+    chip2 = keep2 + got2
+    far2 = swap(chip2, "xl")
+    total_b = jnp.concatenate([chip1 + far1, chip2 + far2], axis=1)
     total_a = swap(total_b, "c")
     xt = band(pos, xa, xb)
 
     logits_a = BETA * (log_prior[:, None] - total_a / D)
     logits_b = BETA * (log_prior[:, None] - total_b / D)
-    h = logits_a.shape[1]
     lse = jnp.concatenate([log_sum(logits_a), log_sum(logits_b)])
     lanes = jnp.broadcast_to(lse.reshape(1, 1, 2 * h), (groups, 1, 2 * h))
     others = lax.all_to_all(lanes, COMP, 0, 0, tiled=True)

time: 97.9 us -> 89.4 us (0.913)
  blocking collectives: 27.3 us -> 0 us
  starting transfers between devices: 4.91 us -> 19.8 us
  waiting for transfers between devices: 18.5 us -> 21.7 us
    all_to_all x1 -> x0, blocking collectives: 27.3 us -> none  [layer(): xa = lax.all_to_all(pieces, CHIPS, 0, 0, tiled=True)]
    all_to_all x0 -> x1, starting transfers between devices: none -> 11.5 us  [layer(): xa = lax.all_to_all(pieces, CHIPS, 0, 0, tiled=True)]
    all_to_all x0 -> x1, waiting for transfers between devices: none -> 7.94 us  [layer(): xa = lax.all_to_all(pieces, CHIPS, 0, 0, tiled=True)]
    ppermute x4 -> x6, waiting for transfers between devices: 8.28 us -> 3.84 us  [swap(): return lax.ppermute(x, axis, [(0, 1), (1, 0)])]
    ppermute x4 -> x6, starting transfers between devices: 0.91 us -> 3.02 us  [swap(): return lax.ppermute(x, axis, [(0, 1), (1, 0)])]
    all_to_all x1, starting transfers between devices: 4 us -> 5.27 us  [layer(): others = lax.all_to_all(lanes, COMP, 0, 0, tiled=True)]
    pallas_call x2 -> x5, Pallas kernels: 18.4 us -> 18.5 us  [the longest x4 18.3 us: dist(): pl.pallas_call(kernel, in_specs=[pl.BlockSpec(memory_space=pl.ANY) if fir...]
  transfers between devices with their start and end apart: 5 -> 8, of which waited for: 3 -> 4; matrix products, arithmetic and copies ran while one was open for 0% -> 0% of each run, Pallas kernels for 26% -> 21%
where the time goes in v4:
time: 89.4 us; the launch traced here: 88.9 us
  Pallas kernels  42.4 us (47%)
  waiting for transfers between devices  21.7 us (24%)
  starting transfers between devices  19.8 us (22%)
  local copies, waits for them, and re-layouts  3.34 us (4%)
    pallas_call x4, Pallas kernels, dist(): pl.pallas_call(kernel, in_specs=[pl.BlockSpec(memory_space=pl.ANY) if fir...  18.3 us
    pallas_call x1, Pallas kernels, sec(): pl.pallas_call(functools.partial(sec_kernel, kb=kb), grid=(k // kb, 2), i...  16.5 us
    all_to_all x1, starting transfers between devices, layer(): xa = lax.all_to_all(pieces, CHIPS, 0, 0, tiled=True)  11.5 us
    all_to_all x1, waiting for transfers between devices, layer(): others = lax.all_to_all(lanes, COMP, 0, 0, tiled=True)  9.93 us
    all_to_all x1, waiting for transfers between devices, layer(): xa = lax.all_to_all(pieces, CHIPS, 0, 0, tiled=True)  7.94 us
    pallas_call x1, Pallas kernels, prep(): pl.pallas_call(functools.partial(prep_kernel, kb=kb), grid_spec=spec, out...  7.19 us
    all_to_all x1, starting transfers between devices, layer(): others = lax.all_to_all(lanes, COMP, 0, 0, tiled=True)  5.27 us
    ppermute x6, waiting for transfers between devices, swap(): return lax.ppermute(x, axis, [(0, 1), (1, 0)])  3.84 us
  transfers between devices with their start and end apart: 8, of which 4 were waited for; matrix products, arithmetic and copies ran while one was open for 0% of the time, Pallas kernels for 21%

profile of v4, /device:TPU:0, one launch (start us, length us, event | category | flops | bytes accessed | tf_op | source)
XLA Modules:
  0.0 88.9 jit_solution(8312060546319072847)
XLA Ops:
  0.6 0.7 broadcast_in_dim.6
  1.4 1.0 %broadcast_in_dim.7 = bf16[64,48,128]{2,1,0:T(8,128)(2,1)} broadcast(bf16[48,128]{1,0:T(8,128)(2,1)S(1)} %broadcast_in_dim.6), dimensions={1,2} | broadcast | bytes 798720 | tf_op jit(solution)/shard_map/broadcast_in_dim | solution.py:250
  2.4 11.5 %all-to-all-start = ((bf16[64,48,128]{2,1,0:T(8,128)(2,1)}), bf16[64,48,128]{2,1,0:T(8,128)(2,1)S(1)}, u32[]{:S(2)}, u32[]{:S(2)}) async-start(bf16[64,48,128]{2,1,0:T(8,128)(2,1)} %broadcast_in_dim.7), calls=%async_computation | async-start | bytes 1572864 | tf_op jit(solution)/shard_map/all_to_all | solution.py:251
  13.9 0.0 copy-start
  13.9 0.8 copy-done
  14.7 7.2 %prep.1 = (f32[8,128,8]{2,1,0:T(8,128)S(1)}, f32[64,128]{1,0:T(8,128)S(1)}) custom-call(s32[1]{0:T(128)} %bitcast.pos, bf16[64,128,512]{2,1,0:T(8,128)(2,1)} %w_hbm.1, bf16[64,128,512]{2,1,0:T(8,128)(2,1)} %w_hbm.1, bf16[64,512]{1,0:T(8,128)(2,1)S(1)} %copy-done), custom_call_target="tpu_custom_call" | custom-call | flops 8000000 | bytes 10500000 | tf_op jit(solution)/shard_map/prep/pallas_call | solution.py:50
  21.9 7.9 %all-to-all-done.g_ref = bf16[64,48,128]{2,1,0:T(8,128)(2,1)S(1)} async-done(((bf16[64,48,128]{2,1,0:T(8,128)(2,1)}), bf16[64,48,128]{2,1,0:T(8,128)(2,1)S(1)}, u32[]{:S(2)}, u32[]{:S(2)}) %all-to-all-start) | async-done | bytes 786464 | tf_op jit(solution)/shard_map/all_to_all | solution.py:251
  29.9 0.2 rows.1.x_ref.xa_ref
  30.1 6.9 %dist_first.1 = (f32[64,512]{1,0:T(8,128)S(1)}, bf16[64,128,512]{2,1,0:T(8,128)(2,1)S(1)}) custom-call(bf16[64,128,512]{2,1,0:T(8,128)(2,1)} %w_hbm.1, f32[8,128,8]{2,1,0:T(8,128)S(1)} %get-tuple-element.12.off_ref, f32[64,128]{1,0:T(8,128)S(1)} %get-tuple-element.13.ld_ref, bf16[768,512]{1,0:T(8,128)(2,1)S(1)} %rows.1.x_ref.xa_ref), custom_call_target="tpu_custom_call" | custom-call | flops 4294967296 | bytes 9043968 | tf_op jit(solution)/shard_map/dist_first/pallas_call | solution.py:110
  37.0 0.1 collective-permute-start
  37.1 3.0 %dist.4 = f32[64,256]{1,0:T(8,128)S(1)} custom-call(bf16[64,128,512]{2,1,0:T(8,128)(2,1)S(1)} %get-tuple-element.14.w_ref, f32[8,128,8]{2,1,0:T(8,128)S(1)} %get-tuple-element.12.off_ref, f32[64,128]{1,0:T(8,128)S(1)} %get-tuple-element.13.ld_ref, bf16[768,512]{1,0:T(8,128)(2,1)S(1)} %rows.1.x_ref.xa_ref), custom_call_target="tpu_custom_call" | custom-call | flops 2147483648 | bytes 8716288 | tf_op jit(solution)/shard_map/dist/pallas_call | solution.py:110
  40.2 0.6 collective-permute-start.3
  40.8 0.1 collective-permute-start.1
  40.9 0.0 collective-permute-done.x_ref.xb_ref
  40.9 5.3 %dist.3 = f32[64,512]{1,0:T(8,128)S(1)} custom-call(bf16[64,128,512]{2,1,0:T(8,128)(2,1)S(1)} %get-tuple-element.14.w_ref, f32[8,128,8]{2,1,0:T(8,128)S(1)} %get-tuple-element.12.off_ref, f32[64,128]{1,0:T(8,128)S(1)} %get-tuple-element.13.ld_ref, bf16[768,512]{1,0:T(8,128)(2,1)S(1)} %collective-permute-done.x_ref.xb_ref), custom_call_target="tpu_custom_call" | custom-call | flops 4294967296 | bytes 9043968 | tf_op jit(solution)/shard_map/dist/pallas_call | solution.py:110
  46.2 0.0 copy-start.1
  46.2 0.1 collective-permute-start.2
  46.3 3.1 %dist.5 = f32[64,256]{1,0:T(8,128)S(1)} custom-call(bf16[64,128,512]{2,1,0:T(8,128)(2,1)S(1)} %get-tuple-element.14.w_ref, f32[8,128,8]{2,1,0:T(8,128)S(1)} %get-tuple-element.12.off_ref, f32[64,128]{1,0:T(8,128)S(1)} %get-tuple-element.13.ld_ref, bf16[768,512]{1,0:T(8,128)(2,1)S(1)} %collective-permute-done.x_ref.xb_ref), custom_call_target="tpu_custom_call" | custom-call | flops 2147483648 | bytes 8716288 | tf_op jit(solution)/shard_map/dist/pallas_call | solution.py:110
  49.4 2.1 %collective-permute-start.4 = (f32[64,256]{1,0:T(8,128)S(1)}, f32[64,256]{1,0:T(8,128)S(1)}, u32[]{:S(2)}, u32[]{:S(2)}) collective-permute-start(f32[64,256]{1,0:T(8,128)S(1)} %add.27), channel_id=1, source_target_pairs={{0,64},{64,0},{1,65},{65,1},{2,66},{66,2},{3,67},{67,3},{4,68},{68... | collective-permute-start | bytes 196616 | tf_op jit(solution)/shard_map/ppermute | solution.py:231
  51.5 2.4 %collective-permute-done.4 = f32[64,256]{1,0:T(8,128)S(1)} collective-permute-done((f32[64,256]{1,0:T(8,128)S(1)}, f32[64,256]{1,0:T(8,128)S(1)}, u32[]{:S(2)}, u32[]{:S(2)}) %collective-permute-start.4) | collective-permute-done | bytes 65568 | tf_op jit(solution)/shard_map/ppermute | solution.py:231
  54.0 0.1 collective-permute-start.5
  54.0 1.4 %collective-permute-done.5 = f32[64,768]{1,0:T(8,128)S(1)} collective-permute-done((f32[64,768]{1,0:T(8,128)S(1)}, f32[64,768]{1,0:T(8,128)S(1)}, u32[]{:S(2)}, u32[]{:S(2)}) %collective-permute-start.5) | collective-permute-done | bytes 196640 | tf_op jit(solution)/shard_map/ppermute | solution.py:231
  55.5 0.1 fusion.2
  55.6 0.1 exponential_reduce_fusion.1
  55.7 0.1 exponential_reduce_fusion
  55.9 0.8 broadcast_in_dim.8
  56.7 5.3 %all-to-all-start.1 = ((f32[32,1,1536]{2,1,0:T(1,128)}), f32[32,1,1536]{2,1,0:T(1,128)S(1)}, u32[]{:S(2)}, u32[]{:S(2)}) async-start(f32[32,1,1536]{2,1,0:T(1,128)} %broadcast_in_dim.8), calls=%async_computation.1 | async-start | bytes 393216 | tf_op jit(solution)/shard_map/all_to_all | solution.py:274
  61.9 0.2 band.1.xt_ref
  62.1 9.9 %all-to-all-done.1 = f32[32,1,1536]{2,1,0:T(1,128)S(1)} async-done(((f32[32,1,1536]{2,1,0:T(1,128)}), f32[32,1,1536]{2,1,0:T(1,128)S(1)}, u32[]{:S(2)}, u32[]{:S(2)}) %all-to-all-start.1) | async-done | bytes 196640 | tf_op jit(solution)/shard_map/all_to_all | solution.py:274
  72.1 0.1 reduce_max.29
  72.3 0.2 exponential_convert_fusion
  72.4 16.5 %sec.1 = (f32[64,128,512]{2,1,0:T(8,128)}, f32[64,512]{1,0:T(8,128)}, f32[1,64]{1,0:T(1,128)}) custom-call(bf16[64,768]{1,0:T(8,128)(2,1)S(1)} %get-tuple-element.26.ra_ref, bf16[64,768]{1,0:T(8,128)(2,1)S(1)} %get-tuple-element.25.rb_ref, bf16[128,1536]{1,0:T(8,128)(2,1)S(1)} %band.1.xt_ref, bf16[768,512]{1,0:T(8,128)(2,1)S(1)} %rows.1.x_ref.xa_ref, ...), custom_call_target="tpu_custom_call" | custom-call | flops 12884901888 | bytes 18350080 | tf_op jit(solution)/shard_map/sec/pallas_call | solution.py:207
  (14 shorter events, 0.2 us)
Async XLA Ops:
  2.4 27.5 %all-to-all-start = ((bf16[64,48,128]{2,1,0:T(8,128)(2,1)}), bf16[64,48,128]{2,1,0:T(8,128)(2,1)S(1)}, u32[]{:S(2)}, u32[]{:S(2)}) async-start(bf16[64,48,128]{2,1,0:T(8,128)(2,1)} %broadcast_in_dim.7), calls=%async_computation | async-start | bytes 1572864 | tf_op jit(solution)/shard_map/all_to_all | solution.py:251
  13.9 0.8 copy-start
  37.0 3.8 %collective-permute-start = (bf16[768,512]{1,0:T(8,128)(2,1)S(1)}, bf16[768,512]{1,0:T(8,128)(2,1)S(1)}, u32[]{:S(2)}, u32[]{:S(2)}) collective-permute-start(bf16[768,512]{1,0:T(8,128)(2,1)S(1)} %rows.1.x_ref.xa_ref), channel_id=1, source_target_pairs={{0,32},{32,0},{1,33},{33,1},{2,34},{34,2},{3,35},{35,3},{4,36},{36... | collective-permute-start | bytes 2359304 | tf_op jit(solution)/shard_map/ppermute | solution.py:231
  40.2 9.2 %collective-permute-start.3 = (f32[64,256]{1,0:T(8,128)S(1)}, f32[64,256]{1,0:T(8,128)S(1)}, u32[]{:S(2)}, u32[]{:S(2)}) collective-permute-start(f32[64,256]{1,0:T(8,128)S(1)} %dist.4), channel_id=1, source_target_pairs={{0,32},{32,0},{1,33},{33,1},{2,34},{34,2},{3,35},{35,3},{4,36},{36... | collective-permute-start | bytes 196616 | tf_op jit(solution)/shard_map/ppermute | solution.py:231
  40.8 5.4 %collective-permute-start.1 = (f32[64,512]{1,0:T(8,128)S(1)}, f32[64,512]{1,0:T(8,128)S(1)}, u32[]{:S(2)}, u32[]{:S(2)}) collective-permute-start(f32[64,512]{1,0:T(8,128)S(1)} %get-tuple-element.17), channel_id=1, source_target_pairs={{0,32},{32,0},{1,33},{33,1},{2,34},{34,2},{3,35},{35,3},{4,36},{36... | collective-permute-start | bytes 393224 | tf_op jit(solution)/shard_map/ppermute | solution.py:231
  46.2 9.3 %copy-start.1 = (f32[64]{0:T(128)S(1)}, f32[64]{0:T(128)}, u32[]{:S(2)}) copy-start(f32[64]{0:T(128)} %param.7) | copy-start | bytes 772
  46.2 7.7 %collective-permute-start.2 = (f32[64,512]{1,0:T(8,128)S(1)}, f32[64,512]{1,0:T(8,128)S(1)}, u32[]{:S(2)}, u32[]{:S(2)}) collective-permute-start(f32[64,512]{1,0:T(8,128)S(1)} %add.25), channel_id=1, source_target_pairs={{0,64},{64,0},{1,65},{65,1},{2,66},{66,2},{3,67},{67,3},{4,68},{68... | collective-permute-start | bytes 393224 | tf_op jit(solution)/shard_map/ppermute | solution.py:231
  49.4 4.5 %collective-permute-start.4 = (f32[64,256]{1,0:T(8,128)S(1)}, f32[64,256]{1,0:T(8,128)S(1)}, u32[]{:S(2)}, u32[]{:S(2)}) collective-permute-start(f32[64,256]{1,0:T(8,128)S(1)} %add.27), channel_id=1, source_target_pairs={{0,64},{64,0},{1,65},{65,1},{2,66},{66,2},{3,67},{67,3},{4,68},{68... | collective-permute-start | bytes 196616 | tf_op jit(solution)/shard_map/ppermute | solution.py:231
  54.0 1.5 %collective-permute-start.5 = (f32[64,768]{1,0:T(8,128)S(1)}, f32[64,768]{1,0:T(8,128)S(1)}, u32[]{:S(2)}, u32[]{:S(2)}) collective-permute-start(f32[64,768]{1,0:T(8,128)S(1)} %pad_maximum_fusion), channel_id=1, source_target_pairs={{0,32},{32,0},{1,33},{33,1},{2,34},{34,2},{3,35},{35,3},{4,36},{36... | collective-permute-start | bytes 589832 | tf_op jit(solution)/shard_map/ppermute | solution.py:231
  56.7 15.4 %all-to-all-start.1 = ((f32[32,1,1536]{2,1,0:T(1,128)}), f32[32,1,1536]{2,1,0:T(1,128)S(1)}, u32[]{:S(2)}, u32[]{:S(2)}) async-start(f32[32,1,1536]{2,1,0:T(1,128)} %broadcast_in_dim.8), calls=%async_computation.1 | async-start | bytes 393216 | tf_op jit(solution)/shard_map/all_to_all | solution.py:274
